TPU v7x, 256 devices: a whole 4x4x8 slice. The times are simulated.
256 devices in a mesh: row: 8 (over z_hi, core), col: 32 (over x, z_lo, y).
Axes of the slice: x: 4, y: 4, z: 8 (z_hi: 4, z_lo: 2; z = z_hi * 2 + z_lo), core: 2. Of those that a mesh axis runs over, the one named last changes fastest.
Arguments:
- basis_out: float32 [16384, 16384], P('row', 'col'), may hold values from -0.046875 to 0.046875
- basis_in: float32 [16384, 16384], P('col', 'row'), may hold values from -0.046875 to 0.046875
- eig_damped: float32 [16384, 16384], P('col', 'row'), may hold values from 0.5 to 8
- query_left: bfloat16 [16384, 256], P(('row', 'col')), may hold values from -0.375 to 0.375
- query_right: bfloat16 [16384, 256], P('col'), may hold values from -6 to 6
- train_left: bfloat16 [16384, 512], P(('row', 'col')), may hold values from -0.046875 to 0.046875
- train_right: bfloat16 [16384, 512], P('col'), may hold values from -0.046875 to 0.046875
Outputs:
- response: float32 [16384, 512], P(('row', 'col'))
- scores: float32 [512], replicated
All inputs are finite; a program needn't handle non-finite values.
Results may differ from a plain program's by a relative error of at most 0.0003.
Values may be sent and summed in bfloat16 or wider, within the bound.
No kernel may reach another device: no remote copies, remote signals or barrier semaphores. Data moves between devices by JAX's collectives and lax.ppermute only.
A program may use at most 128 MiB of HBM per device.

v0:
```python
import jax
import jax.numpy as jnp
from jax import lax
from jax.sharding import Mesh
from jax.sharding import PartitionSpec as P

COL = ("col_0", "col_1", "col_2")
ROW = ("row_0", "row_1")
ROW_COL = ("row_0", "row_1", "col_0", "col_1", "col_2")


def joined_along(pieces, dim):
    dims = list(pieces.shape[1:])
    dims[dim] *= pieces.shape[0]
    return jnp.moveaxis(pieces, 0, dim).reshape(dims)


def from_everyone(array, axis):
    copies = jnp.broadcast_to(array, (lax.axis_size(axis), *array.shape))
    return lax.all_to_all(copies, axis, split_axis=0, concat_axis=0, tiled=True)


def gathered_copies(array, axis, dim):
    return joined_along(from_everyone(array, axis), dim)


def over_copies(array, axis):
    everything = from_everyone(array, axis)
    return jnp.sum(everything, axis=0)


def sum_in_order(pieces, axes, turns):
    dims = [lax.axis_size(a) for a in axes]
    pieces = pieces.reshape(*dims, *pieces.shape[1:])
    pieces = pieces.transpose(*turns, *range(len(axes), pieces.ndim))
    pieces = pieces.reshape(-1, *pieces.shape[len(axes) :])
    for k in turns:
        pieces = lax.psum_scatter(pieces, axes[k], scatter_dimension=0, tiled=True)
    return pieces[0]


def in_blocks(array, dim, devices):
    dims = array.shape
    pieces = array.reshape(*dims[:dim], devices, dims[dim] // devices, *dims[dim + 1 :])
    return jnp.moveaxis(pieces, dim, 0)


def summed_rows(array, axes, turns, dim):
    devices = lax.axis_size(axes)
    return sum_in_order(in_blocks(array, dim, devices), axes, turns)


def sent_and_summed(array, axis, dim):
    pieces = in_blocks(array, dim, lax.axis_size(axis))
    arrived = lax.all_to_all(pieces, axis, split_axis=0, concat_axis=0, tiled=True)
    return arrived.sum(axis=0)


def one_axis_at_a_time(array, axes):
    for axis in axes:
        array = lax.psum(array, axis)
    return array


def dot_first(left, right):
    return lax.dot_general(
        left,
        right,
        (((0,), (0,)), ((), ())),
        precision=lax.Precision.HIGHEST,
        preferred_element_type=jnp.float32,
    )


def dot_last(left, right):
    return lax.dot_general(
        left,
        right,
        (((1,), (1,)), ((), ())),
        precision=lax.Precision.HIGHEST,
        preferred_element_type=jnp.float32,
    )


def dot_plain(left, right):
    return jnp.dot(left, right, precision=lax.Precision.HIGHEST, preferred_element_type=jnp.float32)


def body(basis_out, basis_in, eig_damped, query_left, query_right, train_left, train_right):
    rank_width = query_right.shape[1]
    basis_rows = basis_out
    rot_left = dot_first(basis_rows, gathered_copies(query_left, COL, 0).astype(jnp.float32))
    rot_left = over_copies(rot_left, ROW)
    joined = jnp.concatenate([query_right, train_right], axis=1).astype(jnp.float32)
    share = summed_rows(dot_first(basis_in, joined), COL, (0, 2, 1), 0)
    piece = lax.all_gather(share, COL, axis=0, tiled=True)
    precond = dot_last(rot_left, piece[:, :rank_width]) / eig_damped
    contrib = dot_plain(precond, piece[:, rank_width:])
    applied = lax.psum(contrib, ROW)
    basis_rows = basis_out
    response = sent_and_summed(dot_plain(basis_rows, applied), COL, 0)
    partial_scores = jnp.sum(train_left.astype(jnp.float32) * response, axis=0)
    scores = one_axis_at_a_time(partial_scores, ROW_COL)
    return (response, scores)


def solution(mesh):
    finer = Mesh(mesh.devices.reshape(4, 2, 4, 2, 4), ("row_0", "row_1", "col_0", "col_1", "col_2"))
    placed = (
        P(ROW, COL),
        P(COL, ROW),
        P(COL, ROW),
        P(ROW_COL, None),
        P(COL, None),
        P(ROW_COL, None),
        P(COL, None),
    )
    return jax.shard_map(
        body, mesh=finer, in_specs=placed, out_specs=(P(ROW_COL, None), P()), check_vma=False
    )
```

profile of v0, /device:TPU:8, one launch (start us, length us, event | category | flops | bytes accessed | tf_op | source)
XLA Modules:
  0.0 579.2 jit_solution(16628478993421398997)
XLA Ops:
  7.2 0.0 reduce-scatter.4.cloned.1.call-start
  7.2 9.0 %convolution_bitcast_fusion = f32[2048,768]{0,1:T(8,128)} fusion(f32[512,2048]{1,0:T(8,128)} %param.8, bf16[512,512]{1,0:T(8,128)(2,1)} %param.13, bf16[512,256]{1,0:T(8,128)(2,1)} %param.11), kind=kOutput, calls=%fused_computation.3 | convolution fusion | flops 9665249280 | bytes 11272192 | tf_op jit(solution)/shard_map/dot_general | solution.py:66
  16.2 6.6 %copy.12 = f32[2048,768]{1,0:T(8,128)} copy(f32[2048,768]{0,1:T(8,128)} %convolution_bitcast_fusion) | data formatting | bytes 12582912 | tf_op jit(solution)/shard_map/dot_general | solution.py:66
  22.8 6.1 %copy.13 = f32[4,4,2,64,768]{4,3,2,1,0:T(8,128)} copy(f32[4,4,2,64,768]{4,3,1,2,0:T(8,128)} %bitcast.18) | data formatting | bytes 12582912 | tf_op jit(solution)/shard_map/transpose | solution.py:35
  28.9 0.0 copy-start.3
  28.9 0.0 reduce-scatter.4.cloned.1.call-update
  28.9 0.0 reduce-scatter.6.cloned.1.call-start
  29.0 69.5 %reduce-scatter.4.cloned.1.call-done = f32[8,64,768]{2,1,0:T(8,128)} async-done(((f32[32,64,768]{2,1,0:T(8,128)}), f32[8,64,768]{2,1,0:T(8,128)}) %reduce-scatter.4.cloned.1.call-update) | async-done | bytes 1572880 | tf_op jit(solution)/shard_map/reduce_scatter | solution.py:38
  98.5 0.0 reduce-scatter.6.cloned.1.call-update
  98.5 0.0 reduce-scatter.8.cloned.1.call-start
  98.6 29.4 %reduce-scatter.6.cloned.1.call-done = f32[2,64,768]{2,1,0:T(8,128)} async-done(((f32[8,64,768]{2,1,0:T(8,128)}), f32[2,64,768]{2,1,0:T(8,128)}) %reduce-scatter.6.cloned.1.call-update) | async-done | bytes 393232 | tf_op jit(solution)/shard_map/reduce_scatter | solution.py:38
  127.9 0.0 reduce-scatter.8.cloned.1.call-update
  127.9 0.0 all-gather.3.cloned.1.call-start
  128.0 21.8 %reduce-scatter.8.cloned.1.call-done = f32[1,64,768]{2,1,0:T(8,128)} async-done(((f32[2,64,768]{2,1,0:T(8,128)}), f32[1,64,768]{2,1,0:T(8,128)}) %reduce-scatter.8.cloned.1.call-update) | async-done | bytes 196624 | tf_op jit(solution)/shard_map/reduce_scatter | solution.py:38
  149.8 0.0 all-gather.3.cloned.1.call-update
  149.8 0.0 all-reduce.2.cloned.1.call-start
  149.8 0.0 copy-done.3
  149.8 0.1 broadcast_in_dim.6
  150.0 25.1 %all_to_all.15 = bf16[32,64,256]{2,1,0:T(8,128)(2,1)S(1)} all-to-all(bf16[32,64,256]{2,1,0:T(8,128)(2,1)S(1)} %broadcast_in_dim.6), channel_id=1, replica_groups=mesh['row_0'=4,'row_1'=2,'col_0'=4,'col_1'=2,'col_2'=4] {'col_0','col_1'..., dimensions={0} | all-to-all | bytes 2097152 | tf_op jit(solution)/shard_map/all_to_all | solution.py:20
  175.1 5.7 fusion.9
  180.8 0.4 broadcast_in_dim.7
  181.2 103.8 %all_to_all.16 = f32[8,512,256]{2,1,0:T(8,128)} all-to-all(f32[8,512,256]{2,1,0:T(8,128)S(1)} %broadcast_in_dim.7), channel_id=1, replica_groups=mesh['row_0'=4,'row_1'=2,'col_0'=4,'col_1'=2,'col_2'=4] {'row_0','row_1'}, dimensions={0} | all-to-all | bytes 8388608 | tf_op jit(solution)/shard_map/all_to_all | solution.py:20
  284.9 2.5 reduce_sum.27
  287.5 71.0 %all-gather.3.cloned.1.call-done = f32[1,2048,768]{2,1,0:T(8,128)} async-done(((f32[1,64,768]{2,1,0:T(8,128)}), f32[1,2048,768]{2,1,0:T(8,128)}) %all-gather.3.cloned.1.call-update) | async-done | bytes 6291472 | tf_op jit(solution)/shard_map/all_gather | solution.py:96
  358.4 0.0 copy-start
  358.4 5.6 fusion.3
  364.1 0.0 copy-done
  364.1 10.3 %fusion = f32[512,512]{1,0:T(8,128)} fusion(f32[2048,768]{1,0:T(8,128)S(1)} %bitcast.22, f32[512,2048]{1,0:T(8,128)S(1)} %fusion.3, f32[512,2048]{1,0:T(8,128)} %param.9), kind=kOutput, calls=%fused_computation | convolution fusion | flops 6443499520 | bytes 13631488 | tf_op jit(solution)/shard_map/dot_general | solution.py:86
  374.4 0.0 all-reduce.2.cloned.1.call-update
  374.4 78.1 %all-reduce.2.cloned.1.call-done = f32[512,512]{1,0:T(8,128)} async-done(((f32[512,512]{1,0:T(8,128)}), f32[512,512]{1,0:T(8,128)}) %all-reduce.2.cloned.1.call-update) | async-done | bytes 1048592 | tf_op jit(solution)/shard_map/psum | solution.py:99
  452.6 16.6 %convolution_bitcast_fusion.1 = f32[2048,512]{0,1:T(8,128)} fusion(f32[512,512]{1,0:T(8,128)} %all-reduce.2.cloned.1.call-done, f32[2048,512]{1,0:T(8,128)} %param.7), kind=kOutput, calls=%fused_computation.4 | convolution fusion | flops 6442450944 | bytes 9437184 | tf_op jit(solution)/shard_map/dot_general | solution.py:86
  469.2 5.3 copy.14
  474.6 56.6 %all_to_all.17 = f32[32,64,512]{2,1,0:T(8,128)} all-to-all(f32[32,64,512]{2,1,0:T(8,128)} %bitcast.19), channel_id=1, replica_groups=mesh['row_0'=4,'row_1'=2,'col_0'=4,'col_1'=2,'col_2'=4] {'col_0','col_1'..., dimensions={0} | all-to-all | bytes 8388608 | tf_op jit(solution)/shard_map/all_to_all | solution.py:55
  531.2 0.0 copy-start.2
  531.2 2.6 reduce_sum.28
  533.7 0.0 copy-done.2
  533.7 0.0 copy-start.1
  533.8 10.9 %psum.43 = f32[512]{0:T(512)S(1)} all-reduce(f32[512]{0:T(512)S(1)} %multiply_reduce_fusion), channel_id=1, replica_groups=mesh['row_0'=4,'row_1'=2,'col_0'=4,'col_1'=2,'col_2'=4] {'row_0'}, use_global_device_ids=true, to_apply=%region_7.0 | all-reduce | flops 512 | bytes 4096 | tf_op jit(solution)/shard_map/psum | solution.py:61
  544.7 2.5 psum.44
  547.2 8.7 %psum.45 = f32[512]{0:T(512)S(1)} all-reduce(f32[512]{0:T(512)S(1)} %psum.44), channel_id=1, replica_groups=mesh['row_0'=4,'row_1'=2,'col_0'=4,'col_1'=2,'col_2'=4] {'col_0'}, use_global_device_ids=true, to_apply=%region_9.0 | all-reduce | flops 512 | bytes 4096 | tf_op jit(solution)/shard_map/psum | solution.py:61
  555.9 4.9 psum.46
  560.8 11.8 %psum.47 = f32[512]{0:T(512)} all-reduce(f32[512]{0:T(512)S(1)} %psum.46), channel_id=1, replica_groups=mesh['row_0'=4,'row_1'=2,'col_0'=4,'col_1'=2,'col_2'=4] {'col_2'}, use_global_device_ids=true, to_apply=%region_11.0 | all-reduce | flops 512 | bytes 4096 | tf_op jit(solution)/shard_map/psum | solution.py:61
  572.7 0.0 copy-done.1
  (1 shorter events, 0.0 us)
Async XLA Ops:
  7.2 91.3 %reduce-scatter.4.cloned.1.call-start = ((), (), s32[]{:S(2)}) async-start(), calls=%async_computation.6 | async-start | bytes 7864320 | tf_op jit(solution)/shard_map/reduce_scatter | solution.py:38
  28.9 120.9 %copy-start.3 = (bf16[64,256]{1,0:T(8,128)(2,1)S(1)}, bf16[64,256]{1,0:T(8,128)(2,1)}, u32[]{:S(2)}) copy-start(bf16[64,256]{1,0:T(8,128)(2,1)} %param.10) | copy-start | bytes 98308
  28.9 99.0 %reduce-scatter.6.cloned.1.call-start = ((), (), s32[]{:S(2)}) async-start(), calls=%async_computation.7 | async-start | bytes 1966080 | tf_op jit(solution)/shard_map/reduce_scatter | solution.py:38
  98.5 51.3 %reduce-scatter.8.cloned.1.call-start = ((), (), s32[]{:S(2)}) async-start(), calls=%async_computation.8 | async-start | bytes 589824 | tf_op jit(solution)/shard_map/reduce_scatter | solution.py:38
  127.9 230.5 %all-gather.3.cloned.1.call-start = ((), (), s32[]{:S(2)}) async-start(), calls=%async_computation.10 | async-start | bytes 6488064 | tf_op jit(solution)/shard_map/all_gather | solution.py:96
  149.8 302.8 %all-reduce.2.cloned.1.call-start = ((), (), s32[]{:S(2)}) async-start(), calls=%async_computation.9 | async-start | bytes 2097152 | tf_op jit(solution)/shard_map/psum | solution.py:99
  358.4 5.6 copy-start
  531.2 2.6 copy-start.2
  533.7 38.9 %copy-start.1 = (f32[64,512]{1,0:T(8,128)}, f32[64,512]{1,0:T(8,128)S(1)}, u32[]{:S(2)}) copy-start(f32[64,512]{1,0:T(8,128)S(1)} %reduce_sum.28) | copy-start | bytes 393220
Sparse Core Ops, SparseCore 0:
  29.1 69.3 reduce-scatter.3
  101.0 26.8 reduce-scatter.5
  130.4 19.3 reduce-scatter.7
  151.4 206.9 all-gather.2
  374.6 77.9 all-reduce.1
where the time goes:
time: 580 us; the launch traced here: 579 us
  waiting for transfers between devices  270 us (47%)
  blocking collectives  224 us (39%)
  matrix products  47.3 us (8%)
  local copies, waits for them, and re-layouts  18.6 us (3%)
  between operations  13.9 us (2%)
    all_to_all x2, blocking collectives, from_everyone(): return lax.all_to_all(copies, axis, split_axis=0, concat_axis=0, tiled=True)  129 us
    reduce_scatter x3, waiting for transfers between devices, sum_in_order(): pieces = lax.psum_scatter(pieces, axes[k], scatter_dimension=0, tiled=True)  121 us
    psum x1, waiting for transfers between devices, body(): applied = lax.psum(contrib, ROW)  78.1 us
    all_gather x1, waiting for transfers between devices, body(): piece = lax.all_gather(share, COL, axis=0, tiled=True)  71 us
    all_to_all x1, blocking collectives, sent_and_summed(): lax.all_to_all(pieces, axis, split_axis=0, concat_axis=0, tiled=True)  56.6 us
    psum x5, blocking collectives, one_axis_at_a_time(): array = lax.psum(array, axis)  38.9 us
    dot_general x2, matrix products, dot_plain(): jnp.dot(left, right, precision=lax.Precision.HIGHEST, preferred_element_t...  27 us
    dot_general x2, matrix products, dot_first(): lax.dot_general(left, right, (((0,), (0,)), ((), ())), precision=lax.Prec...  14.7 us
  transfers between devices with their start and end apart: 5, of which 5 were waited for; matrix products, arithmetic and copies ran while one was open for 2% of the time, Pallas kernels for 0%

commit v1 on v0

v1 whole, which is shorter than its diff:
```python
import jax
import jax.numpy as jnp
from jax import lax
from jax.experimental import pallas as pl
from jax.experimental.pallas import tpu as pltpu
from jax.sharding import Mesh
from jax.sharding import PartitionSpec as P

COL = ("col_0", "col_1", "col_2")
ROW = ("row_0", "row_1")
ROW_COL = ROW + COL

SPAN = 250.0
HALF = 125.0
SHARE = 64
f32, bf16 = jnp.float32, jnp.bfloat16


def exchange(pieces, axis):
    return lax.all_to_all(pieces, axis, split_axis=0, concat_axis=0, tiled=True)


def to_everyone(array, axis):
    return exchange(jnp.broadcast_to(array, (lax.axis_size(axis), *array.shape)), axis)


def ring(axis, step):
    n = lax.axis_size(axis)
    return [(k, (k + step) % n) for k in range(n)]


def levels_of(block, axis):
    most = jnp.max(jnp.abs(block), axis=axis, keepdims=True)
    level = jnp.ceil(jnp.log2(jnp.maximum(most, 1e-36)) * 8.0) * 0.125
    return level, jnp.floor(level)


def code_of(block, level):
    size = jnp.exp2(jnp.abs(block) * (jnp.exp2(-level) * SPAN) - HALF)
    return jnp.where(block < 0, -size, size).astype(bf16)


def value_of(code, scale):
    code = code.astype(f32)
    size = (jnp.log2(jnp.abs(code)) + HALF) * scale
    return jnp.where(code < 0, -size, size)


def put_blocks(out, lead, parts):
    rows = jnp.zeros((16, 128), f32)
    at = lax.broadcasted_iota(jnp.int32, (16, 128), 0)
    for k, part in enumerate(parts):
        level, first = levels_of(part, 0)
        out[lead, pl.ds(k * SHARE, SHARE), :] = code_of(part, level)
        rows = jnp.where(at == k, first, rows)
        rows = jnp.where(at == k + 8, level - first, rows)
    out[lead, pl.ds(len(parts) * SHARE, 16), :] = rows.astype(bf16)


def message_of(blocks):
    level, first = levels_of(blocks, 1)
    code = code_of(blocks, level).reshape(-1, 128)
    pad = ((0, 8 - blocks.shape[0]), (0, 0))
    rows = [jnp.pad(a[:, 0], pad).astype(bf16) for a in (first, level - first)]
    return jnp.concatenate([code, *rows], axis=0)


def sum_of(got):
    n = got.shape[1] // SHARE
    level = got[:, n * SHARE : n * SHARE + n].astype(f32) + got[:, -8 : n - 8].astype(f32)
    scale = jnp.exp2(level)[:, :, None] * (1.0 / SPAN)
    return jnp.sum(value_of(got[:, : n * SHARE].reshape(-1, n, SHARE, 128), scale), axis=0)


def halves(array):
    high = array.astype(bf16)
    return high, (array - high.astype(f32)).astype(bf16)


def split(array):
    high = lax.reduce_precision(array, 8, 7)
    return high.astype(bf16), (array - high).astype(bf16)


def multiply(left, right, dims):
    return lax.dot_general(left, right, (dims, ((), ())), preferred_element_type=f32)


FIRST, PLAIN, LAST = ((0,), (0,)), ((1,), (0,)), ((1,), (1,))


def call(kernel, out, grid, ins, outs, args, flops, vmem, scratch=()):
    size = sum(a.size * a.dtype.itemsize for a in args)
    return pl.pallas_call(
        kernel,
        out_shape=out,
        grid=(grid,),
        in_specs=ins,
        out_specs=outs,
        scratch_shapes=scratch,
        cost_estimate=pl.CostEstimate(flops=flops, transcendentals=0, bytes_accessed=size),
        compiler_params=pltpu.CompilerParams(vmem_limit_bytes=vmem * 2**20),
        name=kernel.__name__,
    )(*args)


def whole(shape):
    return pl.BlockSpec(shape, lambda i: (0,) * len(shape))


def blocks(shape, dim):
    return pl.BlockSpec(shape, lambda i: tuple(i if k == dim else 0 for k in range(len(shape))))


def rotate_in(basis, given, out):
    right = jnp.concatenate(halves(basis[...]), axis=0)
    n = out.shape[1] // SHARE
    for h in range(2):
        rows = slice(h * n * SHARE, (h + 1) * n * SHARE)
        turned = multiply(given[rows, :], right, PLAIN)
        for d in range(out.shape[0] // 2):
            cut = slice(d * 128, (d + 1) * 128)
            put_blocks(
                out, 2 * d + h, [turned[k * SHARE : (k + 1) * SHARE, cut] for k in range(n)]
            )


def apply_piece(got, left, eig, out, right, other):
    n = got.shape[1] // SHARE
    tall = right.shape[0] // 3

    @pl.when(pl.program_id(0) == 0)
    def _():
        out[...] = jnp.zeros_like(out)

    for d in range(got.shape[0]):
        rows = got[d, pl.ds(n * SHARE, 16), :].astype(f32)
        lanes = pl.ds((d // 2) * 128, 128)
        for k in range(n):
            scale = jnp.exp2(rows[k : k + 1] + rows[k + 8 : k + 9]) * (1.0 / SPAN)
            high, low = halves(value_of(got[d, pl.ds(k * SHARE, SHARE), :], scale))
            at = ((d % 2) * n + k) * SHARE
            if at < tall:
                right[pl.ds(at, SHARE), lanes] = high
                right[pl.ds(tall + at, SHARE), lanes] = high
                right[pl.ds(2 * tall + at, SHARE), lanes] = low
            else:
                at = pl.ds(at - tall, SHARE)
                wide = eig.shape[1]
                other[at, lanes] = high
                other[at, pl.ds(wide + (d // 2) * 128, 128)] = high
                other[at, pl.ds(2 * wide + (d // 2) * 128, 128)] = low
    high, low = halves(multiply(left[...], right[...], PLAIN) / eig[...])
    out[...] += multiply(jnp.concatenate([high, low, high], axis=1), other[...], LAST)


def respond(basis, given, out):
    high, low = halves(basis[...])
    partial = multiply(jnp.concatenate([high, low, high], axis=1), given[...], PLAIN)
    n = partial.shape[1] // 128
    for d in range(out.shape[0]):
        rows = slice(d * SHARE, (d + 1) * SHARE)
        put_blocks(out, d, [partial[rows, k * 128 : (k + 1) * 128] for k in range(n)])


def my_half_summed(array):
    core = lax.axis_index("row_1")
    rows = array.shape[0] // 2
    mine = lax.dynamic_slice_in_dim(array, core * rows, rows, 0)
    other = lax.dynamic_slice_in_dim(array, (1 - core) * rows, rows, 0)
    return mine + lax.ppermute(other, "row_1", ring("row_1", 1))


def both_halves(half):
    core = lax.axis_index("row_1")
    other = lax.ppermute(half, "row_1", ring("row_1", 1))
    return jnp.where(
        core == 0, jnp.concatenate([half, other], 0), jnp.concatenate([other, half], 0)
    )


def summed_over_chips(array):
    rows, cols = array.shape
    blocks_ = array.reshape(rows // SHARE, SHARE, cols)
    most = jnp.max(jnp.abs(blocks_), axis=1, keepdims=True)
    level = jnp.ceil(jnp.log2(jnp.maximum(most, 1e-36)) * 8.0) * 0.125
    code = code_of(blocks_, level).reshape(rows, cols)
    first = jnp.floor(level)
    levels = jnp.concatenate([first, level - first], axis=1)
    levels = jnp.concatenate([levels, jnp.zeros((rows // SHARE, 14, cols), f32)], axis=1)
    message = jnp.concatenate([code, levels.reshape(-1, cols).astype(bf16)], axis=0)
    total = array
    for step in (2, 1, 3):
        got = lax.ppermute(message, "row_0", ring("row_0", step))
        level = got[rows:].reshape(rows // SHARE, 16, cols)[:, :2].astype(f32)
        scale = jnp.exp2(jnp.sum(level, axis=1, keepdims=True)) * (1.0 / SPAN)
        total += value_of(got[:rows].reshape(blocks_.shape), scale).reshape(rows, cols)
    return total


def body(basis_out, basis_in, eig_damped, query_left, query_right, train_left, train_right):
    cols = lax.axis_size(COL)
    rank, train = query_right.shape[1], train_right.shape[1]
    n_out, n_in = eig_damped.shape
    struct = jax.ShapeDtypeStruct

    query = to_everyone(query_left, COL)
    step = 4
    n = (rank + train) // 128
    height = n * SHARE + 16
    wide = step // 2 * 128
    given = jnp.concatenate([query_right, train_right], axis=1).T
    given = jnp.concatenate([given, given], axis=1)
    message = call(
        rotate_in,
        pltpu.VMEM((cols, height, 128), bf16),
        cols // step,
        [blocks((basis_in.shape[0], wide), 1), whole(given.shape)],
        blocks((step, height, 128), 0),
        (basis_in, given),
        4 * basis_in.size * (rank + train),
        16,
    )
    message, query = lax.optimization_barrier((message, query))
    got = exchange(message, COL)

    high, low = split(basis_out)
    query = query.reshape(-1, rank)
    rot_left = multiply(high, query, FIRST) + multiply(low, query, FIRST)
    rot_left = both_halves(summed_over_chips(my_half_summed(rot_left)))
    high, low = split(rot_left)
    left = jnp.concatenate([high, low, high], axis=1)

    got = to_everyone(message_of(sum_of(got)), COL)
    contrib = call(
        apply_piece,
        struct((n_out, train), f32),
        cols // step,
        [
            blocks((step, height, 128), 0),
            whole(left.shape),
            blocks((n_out, wide), 1),
        ],
        whole((n_out, train)),
        (got, left, eig_damped),
        6 * eig_damped.size * (rank + train),
        24,
        [pltpu.VMEM((3 * rank, wide), bf16), pltpu.VMEM((train, 3 * wide), bf16)],
    )
    applied = both_halves(summed_over_chips(my_half_summed(contrib)))
    high, low = split(applied)
    given = jnp.concatenate([high, high, low], axis=0)

    n = train // 128
    height = n * SHARE + 16
    message = call(
        respond,
        pltpu.VMEM((cols, height, 128), bf16),
        cols // step,
        [blocks((step * SHARE, n_out), 0), whole(given.shape)],
        blocks((step, height, 128), 0),
        (basis_out, given),
        6 * basis_out.size * train,
        16,
    )
    response = sum_of(exchange(message, COL))
    response = jnp.concatenate([response[k] for k in range(n)], axis=1)
    scores = jnp.sum(train_left.astype(f32) * response, axis=0).reshape(-1, 128)
    scores = jnp.sum(to_everyone(scores, COL), axis=0)
    scores = jnp.sum(to_everyone(scores, ROW), axis=0)
    return response, scores.reshape(-1)


def solution(mesh):
    finer = Mesh(mesh.devices.reshape(4, 2, 4, 2, 4), ROW_COL)
    placed = (
        P(ROW, COL),
        P(COL, ROW),
        P(COL, ROW),
        P(ROW_COL, None),
        P(COL, None),
        P(ROW_COL, None),
        P(COL, None),
    )
    return jax.shard_map(
        body, mesh=finer, in_specs=placed, out_specs=(P(ROW_COL, None), P()), check_vma=False
    )
```

time: 580 us -> 267 us (0.46)
  waiting for transfers between devices: 270 us -> 69.9 us
  blocking collectives: 224 us -> 114 us
  matrix products: 47.3 us -> 5.6 us
  starting transfers between devices: 0.19 us -> 30.9 us
  Pallas kernels: 0 us -> 20.5 us
  between operations: 13.9 us -> 1.07 us
  local copies, waits for them, and re-layouts: 18.6 us -> 11.3 us
    reduce_scatter x3 -> x0, waiting for transfers between devices: 121 us -> none  [sum_in_order(): pieces = lax.psum_scatter(pieces, axes[k], scatter_dimension=0, tiled=True)]
    psum x1 -> x0, waiting for transfers between devices: 78.1 us -> none  [body(): applied = lax.psum(contrib, ROW)]
    all_to_all x3 -> x4, blocking collectives: 185 us -> 114 us  [exchange(): return lax.all_to_all(pieces, axis, split_axis=0, concat_axis=0, tiled=True)]
    all_gather x1 -> x0, waiting for transfers between devices: 71 us -> none  [body(): piece = lax.all_gather(share, COL, axis=0, tiled=True)]
    ppermute x0 -> x10, waiting for transfers between devices: none -> 63.4 us  [the longest x6 56.6 us: summed_over_chips(): got = lax.ppermute(message, 'row_0', ring('row_0', step))]
    dot_general x5 -> x2, matrix products: 47.3 us -> 5.6 us  [multiply(): lax.dot_general(left, right, (dims, ((), ())), preferred_element_type=f32)]
    psum x5 -> x0, blocking collectives: 38.9 us -> none  [one_axis_at_a_time(): array = lax.psum(array, axis)]
    pallas_call x0 -> x3, Pallas kernels: none -> 20.5 us  [call(): pl.pallas_call(kernel, out_shape=out, grid=(grid,), in_specs=ins, out_spe...]
  transfers between devices with their start and end apart: 5 -> 12, of which waited for: 5 -> 9; matrix products, arithmetic and copies ran while one was open for 2% -> 4% of each run, Pallas kernels for 0% -> 3%
where the time goes in v1:
time: 267 us; the launch traced here: 264 us
  blocking collectives  114 us (43%)
  waiting for transfers between devices  69.9 us (26%)
  starting transfers between devices  30.9 us (12%)
  Pallas kernels  20.5 us (8%)
  local copies, waits for them, and re-layouts  11.3 us (4%)
  other arithmetic  10.9 us (4%)
  matrix products  5.6 us (2%)
    all_to_all x4, blocking collectives, exchange(): return lax.all_to_all(pieces, axis, split_axis=0, concat_axis=0, tiled=True)  114 us
    ppermute x6, waiting for transfers between devices, summed_over_chips(): got = lax.ppermute(message, 'row_0', ring('row_0', step))  56.6 us
    pallas_call x3, Pallas kernels, call(): pl.pallas_call(kernel, out_shape=out, grid=(grid,), in_specs=ins, out_spe...  20.5 us
    ppermute x6, starting transfers between devices, summed_over_chips(): got = lax.ppermute(message, 'row_0', ring('row_0', step))  16.3 us
    all_to_all x2, starting transfers between devices, exchange(): return lax.all_to_all(pieces, axis, split_axis=0, concat_axis=0, tiled=True)  14 us
    unnamed x20, local copies, waits for them, and re-layouts  7.03 us
    all_to_all x2, waiting for transfers between devices, exchange(): return lax.all_to_all(pieces, axis, split_axis=0, concat_axis=0, tiled=True)  6.45 us
    dot_general x2, matrix products, multiply(): lax.dot_general(left, right, (dims, ((), ())), preferred_element_type=f32)  5.6 us
  transfers between devices with their start and end apart: 12, of which 9 were waited for; matrix products, arithmetic and copies ran while one was open for 4% of the time, Pallas kernels for 3%

profile of v1, /device:TPU:8, one launch (start us, length us, event | category | flops | bytes accessed | tf_op | source)
XLA Modules:
  0.0 264.2 jit_solution(10935489306345110268)
XLA Ops:
  0.7 1.9 broadcast_in_dim.12
  2.6 8.9 %all-to-all-start = ((bf16[32,64,256]{2,1,0:T(8,128)(2,1)}), bf16[32,64,256]{2,1,0:T(8,128)(2,1)}, u32[]{:S(2)}, u32[]{:S(2)}) async-start(bf16[32,64,256]{2,1,0:T(8,128)(2,1)} %broadcast_in_dim.12), calls=%async_computation | async-start | bytes 2097152 | tf_op jit(solution)/shard_map/all_to_all | solution.py:20
  11.5 0.2 copy.16
  11.8 0.1 copy.15
  11.9 0.1 maximum_bitcast_fusion
  12.0 0.2 pad_maximum_fusion.given
  12.2 0.0 copy-start.3
  12.2 2.2 copy-done.3
  14.4 6.9 %rotate_in.1 = bf16[32,400,128]{2,1,0:T(8,128)(2,1)S(1)} custom-call(f32[512,2048]{1,0:T(8,128)S(1)} %copy-done.3, bf16[768,1024]{1,0:T(8,128)(2,1)S(1)} %pad_maximum_fusion.given), custom_call_target="tpu_custom_call" | custom-call | flops 3221225472 | bytes 5767168 | tf_op jit(solution)/shard_map/rotate_in/pallas_call | solution.py:94
  21.3 6.4 %all-to-all-done = bf16[32,64,256]{2,1,0:T(8,128)(2,1)} async-done(((bf16[32,64,256]{2,1,0:T(8,128)(2,1)}), bf16[32,64,256]{2,1,0:T(8,128)(2,1)}, u32[]{:S(2)}, u32[]{:S(2)}) %all-to-all-start) | async-done | bytes 1048608 | tf_op jit(solution)/shard_map/all_to_all | solution.py:20
  27.8 44.3 %all_to_all.30 = bf16[32,400,128]{2,1,0:T(8,128)(2,1)S(1)} all-to-all(bf16[32,400,128]{2,1,0:T(8,128)(2,1)S(1)} %rotate_in.1), channel_id=1, replica_groups=mesh['row_0'=4,'row_1'=2,'col_0'=4,'col_1'=2,'col_2'=4] {'col_0','col_1'..., dimensions={0} | all-to-all | bytes 6553600 | tf_op jit(solution)/shard_map/all_to_all | solution.py:20
  72.1 2.4 fusion.4
  74.6 0.1 fusion.59
  74.7 2.1 broadcast_in_dim.13
  76.8 5.1 %all-to-all-start.2 = ((bf16[32,400,128]{2,1,0:T(8,128)(2,1)}), bf16[32,400,128]{2,1,0:T(8,128)(2,1)S(1)}, u32[]{:S(2)}, u32[]{:S(2)}) async-start(bf16[32,400,128]{2,1,0:T(8,128)(2,1)} %broadcast_in_dim.13), calls=%async_computation.2 | async-start | bytes 6553600 | tf_op jit(solution)/shard_map/all_to_all | solution.py:20
  81.9 0.0 copy-start
  81.9 3.4 %fusion.11 = f32[512,256]{1,0:T(8,128)S(1)} fusion(bf16[2048,256]{1,0:T(8,128)(2,1)} %bitcast.4, f32[2048,512]{1,0:T(8,128)} %basis.3), kind=kOutput, calls=%fused_computation.19 | convolution fusion | flops 540016640 | bytes 5767168 | tf_op jit(solution)/shard_map/dot_general | solution.py:86
  85.3 0.4 copy-done
  85.7 2.2 fusion.15
  87.9 0.8 copy-done.5
  88.7 0.1 collective-permute-start
  88.8 0.1 pad.38.clone
  88.9 1.6 collective-permute-done
  90.5 1.1 bitcast_reduce_fusion.1
  91.6 0.1 fusion.49
  91.7 0.1 maximum_maximum_fusion.1
  91.8 5.5 %collective-permute-start.3 = (bf16[320,256]{1,0:T(8,128)(2,1)S(1)}, bf16[320,256]{1,0:T(8,128)(2,1)S(1)}, u32[]{:S(2)}, u32[]{:S(2)}) collective-permute-start(bf16[320,256]{1,0:T(8,128)(2,1)S(1)} %pad_maximum_fusion.4), channel_id=1, source_target_pairs={{0,192},{64,0},{128,64},{192,128},{1,193},{65,1},{129,65},{193,129... | collective-permute-start | bytes 491528 | tf_op jit(solution)/shard_map/ppermute | solution.py:194
  97.3 0.0 collective-permute-start.2
  97.3 3.8 %collective-permute-start.1 = (bf16[320,256]{1,0:T(8,128)(2,1)S(1)}, bf16[320,256]{1,0:T(8,128)(2,1)S(1)}, u32[]{:S(2)}, u32[]{:S(2)}) collective-permute-start(bf16[320,256]{1,0:T(8,128)(2,1)S(1)} %pad_maximum_fusion.4), channel_id=1, source_target_pairs={{0,128},{64,192},{128,0},{192,64},{1,129},{65,193},{129,1},{193,65... | collective-permute-start | bytes 491528 | tf_op jit(solution)/shard_map/ppermute | solution.py:194
  101.1 0.0 collective-permute-done.3
  101.1 31.6 %collective-permute-done.2 = bf16[320,256]{1,0:T(8,128)(2,1)S(1)} collective-permute-done((bf16[320,256]{1,0:T(8,128)(2,1)S(1)}, bf16[320,256]{1,0:T(8,128)(2,1)S(1)}, u32[]{:S(2)}, u32[]{:S(2)}) %collective-permute-start.2) | collective-permute-done | bytes 163872 | tf_op jit(solution)/shard_map/ppermute | solution.py:194
  132.7 2.6 collective-permute-done.1
  135.3 0.3 fusion.52
  135.6 0.1 collective-permute-start.4
  135.7 1.6 collective-permute-done.4
  137.4 1.1 fusion.29
  138.5 0.9 pad_maximum_fusion.2.left
  139.4 1.1 copy-done.2
  140.6 2.2 copy-done.4
  142.8 7.8 %apply_piece.1 = f32[512,512]{1,0:T(8,128)S(1)} custom-call(bf16[32,400,128]{2,1,0:T(8,128)(2,1)S(1)} %all-to-all-done.2.got, bf16[512,768]{1,0:T(8,128)(2,1)S(1)} %copy-done.2, f32[512,2048]{1,0:T(8,128)S(1)} %copy-done.4), custom_call_target="tpu_custom_call" | custom-call | flops 4831838208 | bytes 8257536 | tf_op jit(solution)/shard_map/apply_piece/pallas_call | solution.py:94
  150.6 0.4 collective-permute-start.5
  151.0 1.8 collective-permute-done.5
  152.8 0.1 bitcast_reduce_fusion
  152.9 0.2 fusion.30
  153.1 0.1 maximum_maximum_fusion
  153.2 2.7 %collective-permute-start.8 = (bf16[320,512]{1,0:T(8,128)(2,1)S(1)}, bf16[320,512]{1,0:T(8,128)(2,1)S(1)}, u32[]{:S(2)}, u32[]{:S(2)}) collective-permute-start(bf16[320,512]{1,0:T(8,128)(2,1)S(1)} %pad_maximum_fusion.3), channel_id=1, source_target_pairs={{0,192},{64,0},{128,64},{192,128},{1,193},{65,1},{129,65},{193,129... | collective-permute-start | bytes 983048 | tf_op jit(solution)/shard_map/ppermute | solution.py:194
  155.9 0.8 collective-permute-start.7
  156.7 3.5 %collective-permute-start.6 = (bf16[320,512]{1,0:T(8,128)(2,1)S(1)}, bf16[320,512]{1,0:T(8,128)(2,1)S(1)}, u32[]{:S(2)}, u32[]{:S(2)}) collective-permute-start(bf16[320,512]{1,0:T(8,128)(2,1)S(1)} %pad_maximum_fusion.3), channel_id=1, source_target_pairs={{0,128},{64,192},{128,0},{192,64},{1,129},{65,193},{129,1},{193,65... | collective-permute-start | bytes 983048 | tf_op jit(solution)/shard_map/ppermute | solution.py:194
  160.2 4.7 %collective-permute-done.8 = bf16[320,512]{1,0:T(8,128)(2,1)S(1)} collective-permute-done((bf16[320,512]{1,0:T(8,128)(2,1)S(1)}, bf16[320,512]{1,0:T(8,128)(2,1)S(1)}, u32[]{:S(2)}, u32[]{:S(2)}) %collective-permute-start.8) | collective-permute-done | bytes 327712 | tf_op jit(solution)/shard_map/ppermute | solution.py:194
  164.9 17.7 %collective-permute-done.7 = bf16[320,512]{1,0:T(8,128)(2,1)S(1)} collective-permute-done((bf16[320,512]{1,0:T(8,128)(2,1)S(1)}, bf16[320,512]{1,0:T(8,128)(2,1)S(1)}, u32[]{:S(2)}, u32[]{:S(2)}) %collective-permute-start.7) | collective-permute-done | bytes 327712 | tf_op jit(solution)/shard_map/ppermute | solution.py:194
  182.8 0.0 copy-start.1
  182.8 0.6 fusion.33
  183.4 0.1 collective-permute-start.9
  183.5 1.9 collective-permute-done.9
  185.4 0.2 reduce-precision_convert_fusion.2
  185.6 0.1 pad_maximum_fusion.1.given
  185.7 5.9 %respond.1 = bf16[32,272,128]{2,1,0:T(8,128)(2,1)S(1)} custom-call(f32[2048,512]{1,0:T(8,128)S(1)} %copy-done.1, bf16[1536,512]{1,0:T(8,128)(2,1)S(1)} %pad_maximum_fusion.1.given), custom_call_target="tpu_custom_call" | custom-call | flops 3221225472 | bytes 5767168 | tf_op jit(solution)/shard_map/respond/pallas_call | solution.py:94
  191.6 0.0 copy-start.8
  191.7 44.2 %all_to_all.31 = bf16[32,272,128]{2,1,0:T(8,128)(2,1)S(1)} all-to-all(bf16[32,272,128]{2,1,0:T(8,128)(2,1)S(1)} %respond.1), channel_id=1, replica_groups=mesh['row_0'=4,'row_1'=2,'col_0'=4,'col_1'=2,'col_2'=4] {'col_0','col_1'..., dimensions={0} | all-to-all | bytes 4456448 | tf_op jit(solution)/shard_map/all_to_all | solution.py:20
  235.9 1.5 fusion.10
  237.5 0.7 multiply_reduce_fusion
  238.2 11.8 %all_to_all.32 = f32[32,4,128]{2,1,0:T(4,128)S(1)} all-to-all(f32[32,4,128]{2,1,0:T(4,128)S(1)} %broadcast_in_dim.16), channel_id=1, replica_groups=mesh['row_0'=4,'row_1'=2,'col_0'=4,'col_1'=2,'col_2'=4] {'col_0','col_1'..., dimensions={0} | all-to-all | bytes 131072 | tf_op jit(solution)/shard_map/all_to_all | solution.py:20
  250.1 13.6 %all_to_all.33 = f32[8,4,128]{2,1,0:T(4,128)S(1)} all-to-all(f32[8,4,128]{2,1,0:T(4,128)S(1)} %broadcast_in_dim.34), channel_id=1, replica_groups=mesh['row_0'=4,'row_1'=2,'col_0'=4,'col_1'=2,'col_2'=4] {'row_0','row_1'}, dimensions={0} | all-to-all | bytes 32768 | tf_op jit(solution)/shard_map/all_to_all | solution.py:20
  263.7 0.6 reduce_sum.109
  (48 shorter events, 0.6 us)
Async XLA Ops:
  0.6 10.9 %copy-start.6 = (bf16[512,512]{1,0:T(8,128)(2,1)S(1)}, bf16[512,512]{1,0:T(8,128)(2,1)}, u32[]{:S(2)}) copy-start(bf16[512,512]{1,0:T(8,128)(2,1)} %param.13) | copy-start | bytes 1572868
  0.6 11.1 %copy-start.7 = (bf16[512,256]{1,0:T(8,128)(2,1)S(1)}, bf16[512,256]{1,0:T(8,128)(2,1)}, u32[]{:S(2)}) copy-start(bf16[512,256]{1,0:T(8,128)(2,1)} %param.11) | copy-start | bytes 786436
  2.6 25.2 %all-to-all-start = ((bf16[32,64,256]{2,1,0:T(8,128)(2,1)}), bf16[32,64,256]{2,1,0:T(8,128)(2,1)}, u32[]{:S(2)}, u32[]{:S(2)}) async-start(bf16[32,64,256]{2,1,0:T(8,128)(2,1)} %broadcast_in_dim.12), calls=%async_computation | async-start | bytes 2097152 | tf_op jit(solution)/shard_map/all_to_all | solution.py:20
  12.2 2.2 copy-start.3
  76.8 62.6 %all-to-all-start.2 = ((bf16[32,400,128]{2,1,0:T(8,128)(2,1)}), bf16[32,400,128]{2,1,0:T(8,128)(2,1)S(1)}, u32[]{:S(2)}, u32[]{:S(2)}) async-start(bf16[32,400,128]{2,1,0:T(8,128)(2,1)} %broadcast_in_dim.13), calls=%async_computation.2 | async-start | bytes 6553600 | tf_op jit(solution)/shard_map/all_to_all | solution.py:20
  81.9 3.8 %copy-start = (f32[2048,512]{1,0:T(8,128)S(1)}, f32[2048,512]{1,0:T(8,128)}, u32[]{:S(2)}) copy-start(f32[2048,512]{1,0:T(8,128)} %basis.3) | copy-start | bytes 12582916
  87.9 0.8 copy-start.5
  88.7 1.8 collective-permute-start
  91.8 9.3 %collective-permute-start.3 = (bf16[320,256]{1,0:T(8,128)(2,1)S(1)}, bf16[320,256]{1,0:T(8,128)(2,1)S(1)}, u32[]{:S(2)}, u32[]{:S(2)}) collective-permute-start(bf16[320,256]{1,0:T(8,128)(2,1)S(1)} %pad_maximum_fusion.4), channel_id=1, source_target_pairs={{0,192},{64,0},{128,64},{192,128},{1,193},{65,1},{129,65},{193,129... | collective-permute-start | bytes 491528 | tf_op jit(solution)/shard_map/ppermute | solution.py:194
  97.3 35.4 %collective-permute-start.2 = (bf16[320,256]{1,0:T(8,128)(2,1)S(1)}, bf16[320,256]{1,0:T(8,128)(2,1)S(1)}, u32[]{:S(2)}, u32[]{:S(2)}) collective-permute-start(bf16[320,256]{1,0:T(8,128)(2,1)S(1)} %pad_maximum_fusion.4), channel_id=1, source_target_pairs={{0,64},{64,128},{128,192},{192,0},{1,65},{65,129},{129,193},{193,1... | collective-permute-start | bytes 491528 | tf_op jit(solution)/shard_map/ppermute | solution.py:194
  97.3 38.0 %collective-permute-start.1 = (bf16[320,256]{1,0:T(8,128)(2,1)S(1)}, bf16[320,256]{1,0:T(8,128)(2,1)S(1)}, u32[]{:S(2)}, u32[]{:S(2)}) collective-permute-start(bf16[320,256]{1,0:T(8,128)(2,1)S(1)} %pad_maximum_fusion.4), channel_id=1, source_target_pairs={{0,128},{64,192},{128,0},{192,64},{1,129},{65,193},{129,1},{193,65... | collective-permute-start | bytes 491528 | tf_op jit(solution)/shard_map/ppermute | solution.py:194
  135.6 1.8 collective-permute-start.4
  139.4 1.1 copy-start.2
  140.6 2.2 copy-start.4
  150.6 2.2 collective-permute-start.5
  153.2 11.6 %collective-permute-start.8 = (bf16[320,512]{1,0:T(8,128)(2,1)S(1)}, bf16[320,512]{1,0:T(8,128)(2,1)S(1)}, u32[]{:S(2)}, u32[]{:S(2)}) collective-permute-start(bf16[320,512]{1,0:T(8,128)(2,1)S(1)} %pad_maximum_fusion.3), channel_id=1, source_target_pairs={{0,192},{64,0},{128,64},{192,128},{1,193},{65,1},{129,65},{193,129... | collective-permute-start | bytes 983048 | tf_op jit(solution)/shard_map/ppermute | solution.py:194
  155.9 26.7 %collective-permute-start.7 = (bf16[320,512]{1,0:T(8,128)(2,1)S(1)}, bf16[320,512]{1,0:T(8,128)(2,1)S(1)}, u32[]{:S(2)}, u32[]{:S(2)}) collective-permute-start(bf16[320,512]{1,0:T(8,128)(2,1)S(1)} %pad_maximum_fusion.3), channel_id=1, source_target_pairs={{0,64},{64,128},{128,192},{192,0},{1,65},{65,129},{129,193},{193,1... | collective-permute-start | bytes 983048 | tf_op jit(solution)/shard_map/ppermute | solution.py:194
  156.7 26.0 %collective-permute-start.6 = (bf16[320,512]{1,0:T(8,128)(2,1)S(1)}, bf16[320,512]{1,0:T(8,128)(2,1)S(1)}, u32[]{:S(2)}, u32[]{:S(2)}) collective-permute-start(bf16[320,512]{1,0:T(8,128)(2,1)S(1)} %pad_maximum_fusion.3), channel_id=1, source_target_pairs={{0,128},{64,192},{128,0},{192,64},{1,129},{65,193},{129,1},{193,65... | collective-permute-start | bytes 983048 | tf_op jit(solution)/shard_map/ppermute | solution.py:194
  182.8 2.9 %copy-start.1 = (f32[2048,512]{1,0:T(8,128)S(1)}, f32[2048,512]{1,0:T(8,128)}, u32[]{:S(2)}) copy-start(f32[2048,512]{1,0:T(8,128)} %basis.3) | copy-start | bytes 12582916
  183.4 2.0 collective-permute-start.9
  191.6 45.8 %copy-start.8 = (bf16[64,512]{1,0:T(8,128)(2,1)S(1)}, bf16[64,512]{1,0:T(8,128)(2,1)}, u32[]{:S(2)}) copy-start(bf16[64,512]{1,0:T(8,128)(2,1)} %param.12) | copy-start | bytes 196612

commit v2 on v1

v2 whole, which is shorter than its diff:
```python
import jax
import jax.numpy as jnp
from jax import lax
from jax.experimental import pallas as pl
from jax.experimental.pallas import tpu as pltpu
from jax.sharding import Mesh
from jax.sharding import PartitionSpec as P

COL = ("col_0", "col_1", "col_2")
ROW = ("row_0", "row_1")
ROW_COL = ROW + COL


SPAN = 250.0
HALF = 125.0
SHARE = 64
f32, bf16 = jnp.float32, jnp.bfloat16


def exchange(pieces, axis):
    return lax.all_to_all(pieces, axis, split_axis=0, concat_axis=0, tiled=True)


def to_everyone(array, axis):
    return exchange(jnp.broadcast_to(array, (lax.axis_size(axis), *array.shape)), axis)


def ring(axis, step):
    n = lax.axis_size(axis)
    return [(k, (k + step) % n) for k in range(n)]


def tail_of(n):
    return 8 if n <= 4 else 16


def levels_of(block, axis):
    most = jnp.max(jnp.abs(block), axis=axis, keepdims=True)
    level = jnp.ceil(jnp.log2(jnp.maximum(most, 1e-36)) * 8.0) * 0.125
    return level, jnp.floor(level)


def code_of(block, level):
    size = jnp.exp2(jnp.abs(block) * (jnp.exp2(-level) * SPAN) - HALF)
    return jnp.where(block < 0, -size, size).astype(bf16)


def value_of(code, scale):
    code = code.astype(f32)
    size = (jnp.log2(jnp.abs(code)) + HALF) * scale
    return jnp.where(code < 0, -size, size)


def put_blocks(out, lead, parts, plain=()):
    tail = tail_of(len(parts))
    out = out.at[lead]
    rows = jnp.zeros((tail, 128), f32)
    at = lax.broadcasted_iota(jnp.int32, (tail, 128), 0)
    for k, part in enumerate(parts):
        level, first = levels_of(part, 0)
        out[pl.ds(k * SHARE, SHARE), :] = code_of(part, level)
        rows = jnp.where(at == k, first, rows)
        rows = jnp.where(at == k + tail // 2, level - first, rows)
    for k, part in enumerate(plain):
        out[pl.ds((len(parts) + k) * SHARE, SHARE), :] = part
    out[pl.ds(out.shape[0] - tail, tail), :] = rows.astype(bf16)


def message_of(blocks):
    level, first = levels_of(blocks, 1)
    code = code_of(blocks, level).reshape(-1, 128)
    pad = ((0, tail_of(blocks.shape[0]) // 2 - blocks.shape[0]), (0, 0))
    rows = [jnp.pad(a[:, 0], pad).astype(bf16) for a in (first, level - first)]
    return jnp.concatenate([code, *rows], axis=0)


def sum_of(got, n):
    at = got.shape[1] - tail_of(n)
    half = at + tail_of(n) // 2
    level = got[:, at : at + n].astype(f32) + got[:, half : half + n].astype(f32)
    scale = jnp.exp2(level)[:, :, None] * (1.0 / SPAN)
    return jnp.sum(value_of(got[:, : n * SHARE].reshape(-1, n, SHARE, 128), scale), axis=0)


def halves(array):
    high = array.astype(bf16)
    return high, (array - high.astype(f32)).astype(bf16)


def split(array):
    high = lax.reduce_precision(array, 8, 7)
    return high.astype(bf16), (array - high).astype(bf16)


def multiply(left, right, dims):
    return lax.dot_general(left, right, (dims, ((), ())), preferred_element_type=f32)


FIRST, PLAIN, LAST = ((0,), (0,)), ((1,), (0,)), ((1,), (1,))


def call(kernel, out, grid, ins, outs, args, flops, vmem, scratch=()):
    size = sum(a.size * a.dtype.itemsize for a in args)
    return pl.pallas_call(
        kernel,
        out_shape=out,
        grid=(grid,),
        in_specs=ins,
        out_specs=outs,
        scratch_shapes=scratch,
        cost_estimate=pl.CostEstimate(flops=flops, transcendentals=0, bytes_accessed=size),
        compiler_params=pltpu.CompilerParams(vmem_limit_bytes=vmem * 2**20),
    )(*args)


def whole(shape):
    return pl.BlockSpec(shape, lambda i: (0,) * len(shape))


def blocks(shape, dim):
    return pl.BlockSpec(shape, lambda i: tuple(i if k == dim else 0 for k in range(len(shape))))


OFFSETS = (0, 3, 1, 2)


def around(array, axis):
    return [array] + [lax.ppermute(array, axis, ring(axis, 4 - k)) for k in OFFSETS[1:]]


def rotate_in(basis, given, query, out):
    right = jnp.concatenate(halves(basis[...]), axis=0)
    n = given.shape[0] // (2 * SHARE)
    plain = [query[:, k * 128 : (k + 1) * 128] for k in range(query.shape[1] // 128)]
    for h in range(2):
        rows = slice(h * n * SHARE, (h + 1) * n * SHARE)
        turned = multiply(given[rows, :], right, PLAIN)
        for d in range(out.shape[2]):
            cut = slice(d * 128, (d + 1) * 128)
            parts = [turned[k * SHARE : (k + 1) * SHARE, cut] for k in range(n)]
            put_blocks(out, (0, h, d), parts, plain)


def apply_piece(place, left, eig, *refs):
    firsts, seconds, (out, right, other, shares, done) = refs[:4], refs[4:8], refs[8:]
    n = (firsts[0].shape[1] - 16) // SHARE
    tall = right.shape[1] // 3
    copies = []
    for s in range(8):
        for t in range(2):
            group = lax.rem(place[0] + OFFSETS[s // 2], 4) * 4
            group += lax.rem(place[1] + OFFSETS[s % 2 * 2 + t], 4)
            lanes = pl.ds(pl.multiple_of(group * 128, 128), 128)
            into = shares.at[s, :, pl.ds(t * 128, 128)]
            copies.append(pltpu.make_async_copy(eig.at[:, lanes], into, done.at[s * 2 + t]))
            copies[-1].start()
    out[...] = jnp.zeros_like(out)
    for s in range(8):
        a, slot = s // 2, s % 2
        for t in range(2):
            b = s % 2 * 2 + t
            lanes = pl.ds(t * 128, 128)
            for h, got in enumerate((firsts[b].at[a], seconds[a].at[b])):
                rows = got[pl.ds(n * SHARE, 16), :].astype(f32)
                for k in range(n):
                    scale = jnp.exp2(rows[k : k + 1] + rows[k + 8 : k + 9]) * (1.0 / SPAN)
                    high, low = halves(value_of(got[pl.ds(k * SHARE, SHARE), :], scale))
                    at = (h * n + k) * SHARE
                    if at < tall:
                        right[slot, pl.ds(at, SHARE), lanes] = high
                        right[slot, pl.ds(tall + at, SHARE), lanes] = high
                        right[slot, pl.ds(2 * tall + at, SHARE), lanes] = low
                    else:
                        at = pl.ds(at - tall, SHARE)
                        other[slot, at, lanes] = high
                        other[slot, at, pl.ds(256 + t * 128, 128)] = high
                        other[slot, at, pl.ds(512 + t * 128, 128)] = low
        copies[2 * s].wait()
        copies[2 * s + 1].wait()
        precond = multiply(left[...], right[slot], PLAIN) / shares[s]
        high, low = halves(precond)
        out[...] += multiply(jnp.concatenate([high, low, high], axis=1), other[slot], LAST)


def respond(basis, given, out):
    high, low = halves(basis[...])
    partial = multiply(jnp.concatenate([high, low, high], axis=1), given[...], PLAIN)
    n = partial.shape[1] // 128
    for d in range(out.shape[0]):
        rows = slice(d * SHARE, (d + 1) * SHARE)
        put_blocks(out, d, [partial[rows, k * 128 : (k + 1) * 128] for k in range(n)])


def my_half_summed(array):
    core = lax.axis_index("row_1")
    rows = array.shape[0] // 2
    mine = lax.dynamic_slice_in_dim(array, core * rows, rows, 0)
    other = lax.dynamic_slice_in_dim(array, (1 - core) * rows, rows, 0)
    return mine + lax.ppermute(other, "row_1", ring("row_1", 1))


def both_halves(half):
    core = lax.axis_index("row_1")
    other = lax.ppermute(half, "row_1", ring("row_1", 1))
    return jnp.where(
        core == 0, jnp.concatenate([half, other], 0), jnp.concatenate([other, half], 0)
    )


def coded_columns(array, tail):
    cols = array.shape[1]
    parts = array.reshape(-1, SHARE, cols)
    level, first = levels_of(parts, 1)
    rows = [code_of(parts, level), first.astype(bf16), (level - first).astype(bf16)]
    rows.append(jnp.zeros((parts.shape[0], tail - 2, cols), bf16))
    return jnp.concatenate(rows, axis=1)


def column_values(message):
    level = message[:, SHARE].astype(f32) + message[:, SHARE + 1].astype(f32)
    return value_of(message[:, :SHARE], jnp.exp2(level)[:, None] * (1.0 / SPAN))


def summed_over_chips(array, after):
    message, _ = lax.optimization_barrier((coded_columns(array, 8), after))
    arrived = [lax.ppermute(message, "row_0", ring("row_0", step)) for step in (1, 3, 2)]
    total = array
    for got in arrived:
        total += column_values(got).reshape(array.shape)
    return total


def summed_in_turn(array):
    me = lax.axis_index("row_0")
    chips = lax.axis_size("row_0")
    message = coded_columns(array, 8)
    total = lax.dynamic_slice_in_dim(array, me * SHARE, SHARE, 0)
    arrived = []
    for step in (1, 3, 2):
        piece = lax.dynamic_index_in_dim(message, lax.rem(me + step, chips), 0)
        arrived.append(lax.ppermute(piece, "row_0", ring("row_0", step)))
    for got in arrived:
        total += column_values(got)[0]
    pieces = lax.all_gather(coded_columns(total, 8), "row_0", axis=0, tiled=True)
    return column_values(pieces).reshape(array.shape)


def respond_to(basis_out, applied):
    cols = lax.axis_size(COL)
    n_out, train = applied.shape
    high, low = split(applied)
    given = jnp.concatenate([high, high, low], axis=0)
    n = train // 128
    height = n * SHARE + tail_of(n)
    step = 4
    message = call(
        respond,
        pltpu.VMEM((cols, height, 128), bf16),
        cols // step,
        [blocks((step * SHARE, n_out), 0), whole(given.shape)],
        blocks((step, height, 128), 0),
        (basis_out, given),
        6 * basis_out.size * train,
        16,
    )
    response = sum_of(exchange(message, COL), n)
    return [response[k] for k in range(n)]


def body(basis_out, basis_in, eig_damped, query_left, query_right, train_left, train_right):
    cols = lax.axis_size(COL)
    rank, train = query_right.shape[1], train_right.shape[1]
    n_out, _ = eig_damped.shape
    struct = jax.ShapeDtypeStruct

    step = 4
    n = (rank + train) // 128
    height = n * SHARE + tail_of(n)
    wide = step // 2 * 128
    given = jnp.concatenate([query_right, train_right], axis=1).T
    given = jnp.concatenate([given, given], axis=1)
    extra = rank // 128 * SHARE
    message = call(
        rotate_in,
        pltpu.VMEM((4, 2, 4, height + extra, 128), bf16),
        cols // step,
        [
            blocks((basis_in.shape[0], wide), 1),
            whole(given.shape),
            whole(query_left.shape),
        ],
        pl.BlockSpec((1, 2, 2, height + extra, 128), lambda i: (i // 2, 0, i % 2, 0, 0)),
        (pltpu.with_memory_space_constraint(basis_in, pltpu.HBM), given, query_left),
        4 * basis_in.size * (rank + train),
        16,
    ).reshape(cols, height + extra, 128)
    got = exchange(message, COL)

    message = message_of(sum_of(got, n))
    other = lax.ppermute(message, "col_1", ring("col_1", 1))
    is_first = lax.axis_index("col_1") == 0
    first = jnp.where(is_first, message, other)
    second = jnp.where(is_first, other, message)
    first, second, got = lax.optimization_barrier((first, second, got))
    firsts = jnp.stack(around(first, "col_0"))
    seconds = jnp.stack(around(second, "col_2"))
    firsts, seconds = lax.optimization_barrier((firsts, seconds))
    pieces = around(firsts, "col_2") + around(seconds, "col_0")

    high, low = split(basis_out)
    query = got[:, n * SHARE : n * SHARE + extra].reshape(cols, -1, SHARE, 128)
    query = query.transpose(0, 2, 1, 3).reshape(cols * SHARE, rank)
    rot_left = multiply(high, query, FIRST) + multiply(low, query, FIRST)
    rot_left = both_halves(summed_over_chips(my_half_summed(rot_left), (firsts, seconds)))
    high, low = split(rot_left)
    left = jnp.concatenate([high, low, high], axis=1)

    place = jnp.stack([lax.axis_index("col_0"), lax.axis_index("col_2")]).astype(jnp.int32)
    contrib = pl.pallas_call(
        apply_piece,
        out_shape=struct((n_out, train), f32),
        in_specs=[pl.BlockSpec(memory_space=pltpu.SMEM)]
        + [pl.BlockSpec(memory_space=k) for k in [pltpu.VMEM, pl.ANY] + [pltpu.VMEM] * 8],
        scratch_shapes=[
            pltpu.VMEM((2, 3 * rank, wide), bf16),
            pltpu.VMEM((2, train, 3 * wide), bf16),
            pltpu.VMEM((8, n_out, 256), f32),
            pltpu.SemaphoreType.DMA((16,)),
        ],
        cost_estimate=pl.CostEstimate(
            flops=6 * eig_damped.size * (rank + train),
            transcendentals=0,
            bytes_accessed=eig_damped.size * 4,
        ),
        compiler_params=pltpu.CompilerParams(vmem_limit_bytes=18 * 2**20),
        name="apply_piece",
    )(place, left, pltpu.with_memory_space_constraint(eig_damped, pltpu.HBM), *pieces)
    applied = both_halves(summed_in_turn(my_half_summed(contrib)))
    response = jnp.concatenate(respond_to(basis_out, applied), axis=1)
    scores = jnp.sum(train_left.astype(f32) * response, axis=0).reshape(-1, 128)
    scores = jnp.sum(to_everyone(scores, COL), axis=0)
    scores = jnp.sum(to_everyone(scores, ROW), axis=0)
    return response, scores.reshape(-1)


def solution(mesh):
    finer = Mesh(mesh.devices.reshape(4, 2, 4, 2, 4), ROW_COL)
    placed = (
        P(ROW, COL),
        P(COL, ROW),
        P(COL, ROW),
        P(ROW_COL, None),
        P(COL, None),
        P(ROW_COL, None),
        P(COL, None),
    )

    return jax.shard_map(
        body, mesh=finer, in_specs=placed, out_specs=(P(ROW_COL, None), P()), check_vma=False
    )
```

time: 267 us -> 265 us (level)
  waiting for transfers between devices: 69.9 us -> 41.5 us
  blocking collectives: 114 us -> 138 us
  starting transfers between devices: 30.9 us -> 37.5 us
  matrix products: 5.6 us -> 1.71 us
  Pallas kernels: 20.5 us -> 23.6 us
    ppermute x6 -> x19, starting transfers between devices: 16.3 us -> 37.2 us  [the longest x12 17.1 us: around(): lax.ppermute(array, axis, ring(axis, 4 - k))]
    ppermute x6 -> x19, waiting for transfers between devices: 56.6 us -> 37.7 us  [the longest x12 21.8 us: around(): lax.ppermute(array, axis, ring(axis, 4 - k))]
    all_gather x0 -> x1, blocking collectives: none -> 14.5 us  [summed_in_turn(): lax.all_gather(coded_columns(total, 8), 'row_0', axis=0, tiled=True)]
    all_to_all x2 -> x0, starting transfers between devices: 14 us -> none  [exchange(): return lax.all_to_all(pieces, axis, split_axis=0, concat_axis=0, tiled=True)]
    all_to_all x4, blocking collectives: 114 us -> 124 us  [exchange(): return lax.all_to_all(pieces, axis, split_axis=0, concat_axis=0, tiled=True)]
    pallas_call x0 -> x1, Pallas kernels: none -> 8.9 us  [body(): pl.pallas_call(apply_piece, out_shape=struct((n_out, train), f32), in_spe...]
    all_to_all x2 -> x0, waiting for transfers between devices: 6.45 us -> none  [exchange(): return lax.all_to_all(pieces, axis, split_axis=0, concat_axis=0, tiled=True)]
    pallas_call x3 -> x2, Pallas kernels: 20.5 us -> 14.7 us  [call(): pl.pallas_call(kernel, out_shape=out, grid=(grid,), in_specs=ins, out_spe...]
  transfers between devices with their start and end apart: 12 -> 23, of which waited for: 9 -> 13; matrix products, arithmetic and copies ran while one was open for 4% -> 2% of each run, Pallas kernels for 3% -> 0%
where the time goes in v2:
time: 265 us; the launch traced here: 262 us
  blocking collectives  138 us (52%)
  waiting for transfers between devices  41.5 us (16%)
  starting transfers between devices  37.5 us (14%)
  Pallas kernels  23.6 us (9%)
  other arithmetic  9.52 us (4%)
  local copies, waits for them, and re-layouts  9.14 us (3%)
    all_to_all x4, blocking collectives, exchange(): return lax.all_to_all(pieces, axis, split_axis=0, concat_axis=0, tiled=True)  124 us
    ppermute x12, waiting for transfers between devices, around(): lax.ppermute(array, axis, ring(axis, 4 - k))  21.8 us
    ppermute x12, starting transfers between devices, around(): lax.ppermute(array, axis, ring(axis, 4 - k))  17.1 us
    pallas_call x2, Pallas kernels, call(): pl.pallas_call(kernel, out_shape=out, grid=(grid,), in_specs=ins, out_spe...  14.7 us
    all_gather x1, blocking collectives, summed_in_turn(): lax.all_gather(coded_columns(total, 8), 'row_0', axis=0, tiled=True)  14.5 us
    ppermute x3, starting transfers between devices, summed_over_chips(): lax.ppermute(message, 'row_0', ring('row_0', step))  10.7 us
    pallas_call x1, Pallas kernels, body(): pl.pallas_call(apply_piece, out_shape=struct((n_out, train), f32), in_spe...  8.9 us
    ppermute x3, starting transfers between devices, summed_in_turn(): arrived.append(lax.ppermute(piece, 'row_0', ring('row_0', step)))  8.53 us
  transfers between devices with their start and end apart: 23, of which 13 were waited for; matrix products, arithmetic and copies ran while one was open for 2% of the time, Pallas kernels for 0%

profile of v2, /device:TPU:8, one launch (start us, length us, event | category | flops | bytes accessed | tf_op | source)
XLA Modules:
  0.0 262.4 jit_solution(12887314375949749580)
XLA Ops:
  0.6 1.3 copy.28
  1.9 1.1 copy.27
  3.1 0.2 pad_maximum_fusion.given
  3.3 8.7 %shard_map.86 = bf16[4,2,4,528,128]{4,3,2,1,0:T(8,128)(2,1)S(1)} custom-call(f32[512,2048]{1,0:T(8,128)} %basis.2, bf16[768,1024]{1,0:T(8,128)(2,1)S(1)} %pad_maximum_fusion.given, bf16[64,256]{1,0:T(8,128)(2,1)S(1)} %copy-done.6), custom_call_target="tpu_custom_call" | custom-call | flops 3221225472 | bytes 5799936 | tf_op jit(solution)/shard_map/pallas_call | solution.py:104
  12.0 60.5 %all_to_all.20 = bf16[32,528,128]{2,1,0:T(8,128)(2,1)S(1)} all-to-all(bf16[32,528,128]{2,1,0:T(8,128)(2,1)S(1)} %bitcast.116), channel_id=1, replica_groups=mesh['row_0'=4,'row_1'=2,'col_0'=4,'col_1'=2,'col_2'=4] {'col_0','col_1'..., dimensions={0} | all-to-all | bytes 8650752 | tf_op jit(solution)/shard_map/all_to_all | solution.py:21
  72.6 2.0 copy-done.7
  74.5 2.4 fusion.4
  77.1 0.8 collective-permute-start
  77.9 4.0 %collective-permute-done = bf16[400,128]{1,0:T(8,128)(2,1)S(1)} collective-permute-done((bf16[400,128]{1,0:T(8,128)(2,1)S(1)}, bf16[400,128]{1,0:T(8,128)(2,1)S(1)}, u32[]{:S(2)}, u32[]{:S(2)}) %collective-permute-start) | collective-permute-done | bytes 102432 | tf_op jit(solution)/shard_map/ppermute | solution.py:300
  81.9 0.7 collective-permute-start.5
  82.6 1.4 collective-permute-start.6
  84.0 1.7 collective-permute-start.7
  85.7 1.1 copy.29
  86.8 0.7 fusion.11
  87.6 1.0 fusion.15
  88.8 0.5 collective-permute-start.2
  89.3 2.7 %collective-permute-start.3 = (bf16[400,128]{1,0:T(8,128)(2,1)S(1)}, bf16[400,128]{1,0:T(8,128)(2,1)S(1)}, u32[]{:S(2)}, u32[]{:S(2)}) collective-permute-start(bf16[400,128]{1,0:T(8,128)(2,1)S(1)} %get-tuple-element.9), channel_id=1, source_target_pairs={{0,24},{8,0},{16,8},{24,16},{1,25},{9,1},{17,9},{25,17},{2,26},{10... | collective-permute-start | bytes 307208 | tf_op jit(solution)/shard_map/ppermute | solution.py:128
  92.1 3.2 %collective-permute-done.2 = bf16[400,128]{1,0:T(8,128)(2,1)S(1)} collective-permute-done((bf16[400,128]{1,0:T(8,128)(2,1)S(1)}, bf16[400,128]{1,0:T(8,128)(2,1)S(1)}, u32[]{:S(2)}, u32[]{:S(2)}) %collective-permute-start.2) | collective-permute-done | bytes 102432 | tf_op jit(solution)/shard_map/ppermute | solution.py:128
  95.3 1.5 collective-permute-done.3
  96.7 1.5 collective-permute-done.4
  98.4 0.1 fusion.42
  98.7 3.6 %collective-permute-start.8 = (bf16[4,72,256]{2,1,0:T(8,128)(2,1)S(1)}, bf16[4,72,256]{2,1,0:T(8,128)(2,1)S(1)}, u32[]{:S(2)}, u32[]{:S(2)}) collective-permute-start(bf16[4,72,256]{2,1,0:T(8,128)(2,1)S(1)} %maximum_maximum_fusion.1), channel_id=1, source_target_pairs={{0,64},{64,128},{128,192},{192,0},{1,65},{65,129},{129,193},{193,1... | collective-permute-start | bytes 442376 | tf_op jit(solution)/shard_map/ppermute | solution.py:226
  102.2 2.6 %collective-permute-start.12 = (bf16[4,400,128]{2,1,0:T(8,128)(2,1)S(1)}, bf16[4,400,128]{2,1,0:T(8,128)(2,1)S(1)}, u32[]{:S(2)}, u32[]{:S(2)}) collective-permute-start(bf16[4,400,128]{2,1,0:T(8,128)(2,1)S(1)} %pad_maximum_fusion.3.refs_0_), channel_id=1, source_target_pairs={{0,1},{1,2},{2,3},{3,0},{4,5},{5,6},{6,7},{7,4},{8,9},{9,10},{10,1... | collective-permute-start | bytes 1228808 | tf_op jit(solution)/shard_map/ppermute | solution.py:128
  104.8 2.2 collective-permute-start.9
  107.1 4.9 %collective-permute-start.10 = (bf16[4,72,256]{2,1,0:T(8,128)(2,1)S(1)}, bf16[4,72,256]{2,1,0:T(8,128)(2,1)S(1)}, u32[]{:S(2)}, u32[]{:S(2)}) collective-permute-start(bf16[4,72,256]{2,1,0:T(8,128)(2,1)S(1)} %maximum_maximum_fusion.1), channel_id=1, source_target_pairs={{0,128},{64,192},{128,0},{192,64},{1,129},{65,193},{129,1},{193,65... | collective-permute-start | bytes 442376 | tf_op jit(solution)/shard_map/ppermute | solution.py:226
  112.0 5.9 %collective-permute-done.9 = bf16[4,72,256]{2,1,0:T(8,128)(2,1)S(1)} collective-permute-done((bf16[4,72,256]{2,1,0:T(8,128)(2,1)S(1)}, bf16[4,72,256]{2,1,0:T(8,128)(2,1)S(1)}, u32[]{:S(2)}, u32[]{:S(2)}) %collective-permute-start.9) | collective-permute-done | bytes 147488 | tf_op jit(solution)/shard_map/ppermute | solution.py:226
  118.0 0.1 negate_select_fusion.6
  118.2 0.1 negate_select_fusion.4
  118.5 1.3 collective-permute-start.13
  119.8 1.8 collective-permute-start.14
  121.6 0.4 collective-permute-start.15
  122.0 2.8 %collective-permute-start.16 = (bf16[4,400,128]{2,1,0:T(8,128)(2,1)S(1)}, bf16[4,400,128]{2,1,0:T(8,128)(2,1)S(1)}, u32[]{:S(2)}, u32[]{:S(2)}) collective-permute-start(bf16[4,400,128]{2,1,0:T(8,128)(2,1)S(1)} %pad_maximum_fusion.4.refs_4_), channel_id=1, source_target_pairs={{0,24},{8,0},{16,8},{24,16},{1,25},{9,1},{17,9},{25,17},{2,26},{10... | collective-permute-start | bytes 1228808 | tf_op jit(solution)/shard_map/ppermute | solution.py:128
  124.9 1.1 collective-permute-start.17
  126.1 1.3 fusion.25
  127.5 2.9 %collective-permute-done.13.refs_2_ = bf16[4,400,128]{2,1,0:T(8,128)(2,1)S(1)} collective-permute-done((bf16[4,400,128]{2,1,0:T(8,128)(2,1)S(1)}, bf16[4,400,128]{2,1,0:T(8,128)(2,1)S(1)}, u32[]{:S(2)}, u32[]{:S(2)}) %collective-permute-start.13) | collective-permute-done | bytes 409632 | tf_op jit(solution)/shard_map/ppermute | solution.py:128
  130.3 10.0 %collective-permute-done.14.refs_3_ = bf16[4,400,128]{2,1,0:T(8,128)(2,1)S(1)} collective-permute-done((bf16[4,400,128]{2,1,0:T(8,128)(2,1)S(1)}, bf16[4,400,128]{2,1,0:T(8,128)(2,1)S(1)}, u32[]{:S(2)}, u32[]{:S(2)}) %collective-permute-start.14) | collective-permute-done | bytes 409632 | tf_op jit(solution)/shard_map/ppermute | solution.py:128
  140.3 1.9 collective-permute-done.16.refs_6_
  142.3 0.7 copy-done.2
  143.0 0.9 collective-permute-done.17.refs_7_
  143.9 0.7 copy-done.4
  144.6 1.0 copy-done.3
  145.6 1.0 copy-done.5
  146.6 8.9 %apply_piece.1 = f32[512,512]{1,0:T(8,128)S(1)} custom-call(s32[2]{0:T(128)S(1)} %pad_add_fusion.place, bf16[512,768]{1,0:T(8,128)(2,1)S(1)} %pad_maximum_fusion.2.left, f32[512,2048]{1,0:T(8,128)} %eig.1, bf16[4,400,128]{2,1,0:T(8,128)(2,1)S(1)} %pad_maximum_fusion.3.refs_0_, bf16[4,400,128]{2,1,0:T(8,128)(2,1)S(1)} %collective-permute-done.12.refs_1_, ...), custom_call_target="tpu_custom_call" | custom-call | flops 4831838208 | bytes 4194304 | tf_op jit(solution)/shard_map/apply_piece/pallas_call | solution.py:319
  155.7 1.9 collective-permute-done.18
  157.6 0.1 broadcast_compare_fusion
  157.8 0.2 fusion.26
  158.0 0.1 maximum_maximum_fusion
  158.2 4.9 %collective-permute-start.19 = (bf16[1,72,512]{2,1,0:T(8,128)(2,1)S(1)}, bf16[1,72,512]{2,1,0:T(8,128)(2,1)S(1)}, u32[]{:S(2)}, u32[]{:S(2)}) collective-permute-start(bf16[1,72,512]{2,1,0:T(8,128)(2,1)S(1)} %get-tuple-element.26), channel_id=1, source_target_pairs={{0,64},{64,128},{128,192},{192,0},{1,65},{65,129},{129,193},{193,1... | collective-permute-start | bytes 221192 | tf_op jit(solution)/shard_map/ppermute | solution.py:241
  163.0 3.7 %collective-permute-start.21 = (bf16[1,72,512]{2,1,0:T(8,128)(2,1)S(1)}, bf16[1,72,512]{2,1,0:T(8,128)(2,1)S(1)}, u32[]{:S(2)}, u32[]{:S(2)}) collective-permute-start(bf16[1,72,512]{2,1,0:T(8,128)(2,1)S(1)} %get-tuple-element.27), channel_id=1, source_target_pairs={{0,128},{64,192},{128,0},{192,64},{1,129},{65,193},{129,1},{193,65... | collective-permute-start | bytes 221192 | tf_op jit(solution)/shard_map/ppermute | solution.py:241
  166.7 2.4 collective-permute-done.20
  169.2 3.6 %collective-permute-done.21 = bf16[1,72,512]{2,1,0:T(8,128)(2,1)S(1)} collective-permute-done((bf16[1,72,512]{2,1,0:T(8,128)(2,1)S(1)}, bf16[1,72,512]{2,1,0:T(8,128)(2,1)S(1)}, u32[]{:S(2)}, u32[]{:S(2)}) %collective-permute-start.21) | collective-permute-done | bytes 73760 | tf_op jit(solution)/shard_map/ppermute | solution.py:241
  172.8 0.2 abs_reduce_fusion
  173.1 14.5 %all_gather.3 = bf16[4,72,512]{2,1,0:T(8,128)(2,1)S(1)} all-gather(bf16[1,72,512]{2,1,0:T(8,128)(2,1)S(1)} %maximum_maximum_fusion.2), channel_id=1, replica_groups=mesh['row_0'=4,'row_1'=2,'col_0'=4,'col_1'=2,'col_2'=4] {'row_0'}, dimensions={0}, use_global_device_ids=true | all-gather | bytes 368640 | tf_op jit(solution)/shard_map/all_gather | solution.py:244
  187.7 0.2 negate_select_fusion.2
  187.9 1.9 collective-permute-done.22
  189.8 0.2 reduce-precision_convert_fusion.2
  190.1 0.1 pad_maximum_fusion.1.given
  190.2 6.0 %shard_map.87 = bf16[32,264,128]{2,1,0:T(8,128)(2,1)S(1)} custom-call(f32[2048,512]{1,0:T(8,128)S(1)} %copy-done.1, bf16[1536,512]{1,0:T(8,128)(2,1)S(1)} %pad_maximum_fusion.1.given), custom_call_target="tpu_custom_call" | custom-call | flops 3221225472 | bytes 5767168 | tf_op jit(solution)/shard_map/pallas_call | solution.py:104
  196.2 39.4 %all_to_all.21 = bf16[32,264,128]{2,1,0:T(8,128)(2,1)S(1)} all-to-all(bf16[32,264,128]{2,1,0:T(8,128)(2,1)S(1)} %shard_map.87), channel_id=1, replica_groups=mesh['row_0'=4,'row_1'=2,'col_0'=4,'col_1'=2,'col_2'=4] {'col_0','col_1'..., dimensions={0} | all-to-all | bytes 4325376 | tf_op jit(solution)/shard_map/all_to_all | solution.py:21
  235.6 1.5 fusion.10
  237.2 0.7 multiply_reduce_fusion
  237.9 11.8 %all_to_all.22 = f32[32,4,128]{2,1,0:T(4,128)S(1)} all-to-all(f32[32,4,128]{2,1,0:T(4,128)S(1)} %broadcast_in_dim.13), channel_id=1, replica_groups=mesh['row_0'=4,'row_1'=2,'col_0'=4,'col_1'=2,'col_2'=4] {'col_0','col_1'..., dimensions={0} | all-to-all | bytes 131072 | tf_op jit(solution)/shard_map/all_to_all | solution.py:21
  249.8 12.1 %all_to_all.23 = f32[8,4,128]{2,1,0:T(4,128)S(1)} all-to-all(f32[8,4,128]{2,1,0:T(4,128)S(1)} %broadcast_in_dim.14), channel_id=1, replica_groups=mesh['row_0'=4,'row_1'=2,'col_0'=4,'col_1'=2,'col_2'=4] {'row_0','row_1'}, dimensions={0} | all-to-all | bytes 32768 | tf_op jit(solution)/shard_map/all_to_all | solution.py:21
  261.9 0.6 reduce_sum.49
  (80 shorter events, 2.0 us)
Async XLA Ops:
  0.6 2.7 %copy-start.6 = (bf16[64,256]{1,0:T(8,128)(2,1)S(1)}, bf16[64,256]{1,0:T(8,128)(2,1)}, u32[]{:S(2)}) copy-start(bf16[64,256]{1,0:T(8,128)(2,1)} %query.1) | copy-start | bytes 98308
  72.5 2.0 copy-start.7
  77.0 8.7 %slice-start = ((bf16[32,528,128]{2,1,0:T(8,128)(2,1)}), bf16[32,128,128]{2,1,0:T(8,128)(2,1)S(1)}, s32[]{:S(2)}) async-start(bf16[32,528,128]{2,1,0:T(8,128)(2,1)} %copy-done.7), calls=%async_computation.4 | async-start | bytes 2097152 | tf_op jit(solution)/shard_map/slice | solution.py:311
  77.1 4.7 %collective-permute-start = (bf16[400,128]{1,0:T(8,128)(2,1)S(1)}, bf16[400,128]{1,0:T(8,128)(2,1)S(1)}, u32[]{:S(2)}, u32[]{:S(2)}) collective-permute-start(bf16[400,128]{1,0:T(8,128)(2,1)S(1)} %fusion.73), channel_id=1, source_target_pairs={{0,4},{4,0},{1,5},{5,1},{2,6},{6,2},{3,7},{7,3},{8,12},{12,8},{9,1... | collective-permute-start | bytes 307208 | tf_op jit(solution)/shard_map/ppermute | solution.py:300
  77.9 8.9 %copy-start = (f32[2048,512]{1,0:T(8,128)S(1)}, f32[2048,512]{1,0:T(8,128)}, u32[]{:S(2)}) copy-start(f32[2048,512]{1,0:T(8,128)} %basis.3) | copy-start | bytes 12582916
  81.9 7.3 %collective-permute-start.5 = (bf16[400,128]{1,0:T(8,128)(2,1)S(1)}, bf16[400,128]{1,0:T(8,128)(2,1)S(1)}, u32[]{:S(2)}, u32[]{:S(2)}) collective-permute-start(bf16[400,128]{1,0:T(8,128)(2,1)S(1)} %get-tuple-element.10), channel_id=1, source_target_pairs={{0,1},{1,2},{2,3},{3,0},{4,5},{5,6},{6,7},{7,4},{8,9},{9,10},{10,1... | collective-permute-start | bytes 307208 | tf_op jit(solution)/shard_map/ppermute | solution.py:128
  82.6 9.4 %collective-permute-start.6 = (bf16[400,128]{1,0:T(8,128)(2,1)S(1)}, bf16[400,128]{1,0:T(8,128)(2,1)S(1)}, u32[]{:S(2)}, u32[]{:S(2)}) collective-permute-start(bf16[400,128]{1,0:T(8,128)(2,1)S(1)} %get-tuple-element.10), channel_id=1, source_target_pairs={{0,3},{1,0},{2,1},{3,2},{4,7},{5,4},{6,5},{7,6},{8,11},{9,8},{10,9... | collective-permute-start | bytes 307208 | tf_op jit(solution)/shard_map/ppermute | solution.py:128
  84.0 8.0 %collective-permute-start.7 = (bf16[400,128]{1,0:T(8,128)(2,1)S(1)}, bf16[400,128]{1,0:T(8,128)(2,1)S(1)}, u32[]{:S(2)}, u32[]{:S(2)}) collective-permute-start(bf16[400,128]{1,0:T(8,128)(2,1)S(1)} %get-tuple-element.10), channel_id=1, source_target_pairs={{0,2},{1,3},{2,0},{3,1},{4,6},{5,7},{6,4},{7,5},{8,10},{9,11},{10,... | collective-permute-start | bytes 307208 | tf_op jit(solution)/shard_map/ppermute | solution.py:128
  88.6 9.7 %collective-permute-start.1 = (f32[256,256]{1,0:T(8,128)S(1)}, f32[256,256]{1,0:T(8,128)S(1)}, u32[]{:S(2)}, u32[]{:S(2)}) collective-permute-start(f32[256,256]{1,0:T(8,128)S(1)} %constant_dynamic-slice_fusion.4), channel_id=1, source_target_pairs={{0,32},{32,0},{1,33},{33,1},{2,34},{34,2},{3,35},{35,3},{4,36},{36... | collective-permute-start | bytes 786440 | tf_op jit(solution)/shard_map/ppermute | solution.py:199
  88.8 6.5 %collective-permute-start.2 = (bf16[400,128]{1,0:T(8,128)(2,1)S(1)}, bf16[400,128]{1,0:T(8,128)(2,1)S(1)}, u32[]{:S(2)}, u32[]{:S(2)}) collective-permute-start(bf16[400,128]{1,0:T(8,128)(2,1)S(1)} %get-tuple-element.9), channel_id=1, source_target_pairs={{0,8},{8,16},{16,24},{24,0},{1,9},{9,17},{17,25},{25,1},{2,10},{10... | collective-permute-start | bytes 307208 | tf_op jit(solution)/shard_map/ppermute | solution.py:128
  89.3 7.5 %collective-permute-start.3 = (bf16[400,128]{1,0:T(8,128)(2,1)S(1)}, bf16[400,128]{1,0:T(8,128)(2,1)S(1)}, u32[]{:S(2)}, u32[]{:S(2)}) collective-permute-start(bf16[400,128]{1,0:T(8,128)(2,1)S(1)} %get-tuple-element.9), channel_id=1, source_target_pairs={{0,24},{8,0},{16,8},{24,16},{1,25},{9,1},{17,9},{25,17},{2,26},{10... | collective-permute-start | bytes 307208 | tf_op jit(solution)/shard_map/ppermute | solution.py:128
  92.0 6.2 %collective-permute-start.4 = (bf16[400,128]{1,0:T(8,128)(2,1)S(1)}, bf16[400,128]{1,0:T(8,128)(2,1)S(1)}, u32[]{:S(2)}, u32[]{:S(2)}) collective-permute-start(bf16[400,128]{1,0:T(8,128)(2,1)S(1)} %get-tuple-element.9), channel_id=1, source_target_pairs={{0,16},{8,24},{16,0},{24,8},{1,17},{9,25},{17,1},{25,9},{2,18},{10... | collective-permute-start | bytes 307208 | tf_op jit(solution)/shard_map/ppermute | solution.py:128
  98.7 13.3 %collective-permute-start.8 = (bf16[4,72,256]{2,1,0:T(8,128)(2,1)S(1)}, bf16[4,72,256]{2,1,0:T(8,128)(2,1)S(1)}, u32[]{:S(2)}, u32[]{:S(2)}) collective-permute-start(bf16[4,72,256]{2,1,0:T(8,128)(2,1)S(1)} %maximum_maximum_fusion.1), channel_id=1, source_target_pairs={{0,64},{64,128},{128,192},{192,0},{1,65},{65,129},{129,193},{193,1... | collective-permute-start | bytes 442376 | tf_op jit(solution)/shard_map/ppermute | solution.py:226
  102.2 19.8 %collective-permute-start.12 = (bf16[4,400,128]{2,1,0:T(8,128)(2,1)S(1)}, bf16[4,400,128]{2,1,0:T(8,128)(2,1)S(1)}, u32[]{:S(2)}, u32[]{:S(2)}) collective-permute-start(bf16[4,400,128]{2,1,0:T(8,128)(2,1)S(1)} %pad_maximum_fusion.3.refs_0_), channel_id=1, source_target_pairs={{0,1},{1,2},{2,3},{3,0},{4,5},{5,6},{6,7},{7,4},{8,9},{9,10},{10,1... | collective-permute-start | bytes 1228808 | tf_op jit(solution)/shard_map/ppermute | solution.py:128
  104.8 13.1 %collective-permute-start.9 = (bf16[4,72,256]{2,1,0:T(8,128)(2,1)S(1)}, bf16[4,72,256]{2,1,0:T(8,128)(2,1)S(1)}, u32[]{:S(2)}, u32[]{:S(2)}) collective-permute-start(bf16[4,72,256]{2,1,0:T(8,128)(2,1)S(1)} %maximum_maximum_fusion.1), channel_id=1, source_target_pairs={{0,192},{64,0},{128,64},{192,128},{1,193},{65,1},{129,65},{193,129... | collective-permute-start | bytes 442376 | tf_op jit(solution)/shard_map/ppermute | solution.py:226
  107.1 10.9 %collective-permute-start.10 = (bf16[4,72,256]{2,1,0:T(8,128)(2,1)S(1)}, bf16[4,72,256]{2,1,0:T(8,128)(2,1)S(1)}, u32[]{:S(2)}, u32[]{:S(2)}) collective-permute-start(bf16[4,72,256]{2,1,0:T(8,128)(2,1)S(1)} %maximum_maximum_fusion.1), channel_id=1, source_target_pairs={{0,128},{64,192},{128,0},{192,64},{1,129},{65,193},{129,1},{193,65... | collective-permute-start | bytes 442376 | tf_op jit(solution)/shard_map/ppermute | solution.py:226
  118.4 6.5 %copy-start.8 = (f32[256,256]{1,0:T(8,128)}, f32[256,256]{1,0:T(8,128)S(1)}, u32[]{:S(2)}) copy-start(f32[256,256]{1,0:T(8,128)S(1)} %bitcast_add_fusion) | copy-start | bytes 786436
  118.4 6.5 %collective-permute-start.11 = (f32[256,256]{1,0:T(8,128)S(1)}, f32[256,256]{1,0:T(8,128)}, u32[]{:S(2)}, u32[]{:S(2)}) collective-permute-start(f32[256,256]{1,0:T(8,128)S(1)} %bitcast_add_fusion), channel_id=1, source_target_pairs={{0,32},{32,0},{1,33},{33,1},{2,34},{34,2},{3,35},{35,3},{4,36},{36... | collective-permute-start | bytes 786440 | tf_op jit(solution)/shard_map/ppermute | solution.py:204
  118.5 11.9 %collective-permute-start.13 = (bf16[4,400,128]{2,1,0:T(8,128)(2,1)S(1)}, bf16[4,400,128]{2,1,0:T(8,128)(2,1)S(1)}, u32[]{:S(2)}, u32[]{:S(2)}) collective-permute-start(bf16[4,400,128]{2,1,0:T(8,128)(2,1)S(1)} %pad_maximum_fusion.3.refs_0_), channel_id=1, source_target_pairs={{0,3},{1,0},{2,1},{3,2},{4,7},{5,4},{6,5},{7,6},{8,11},{9,8},{10,9... | collective-permute-start | bytes 1228808 | tf_op jit(solution)/shard_map/ppermute | solution.py:128
  119.8 20.6 %collective-permute-start.14 = (bf16[4,400,128]{2,1,0:T(8,128)(2,1)S(1)}, bf16[4,400,128]{2,1,0:T(8,128)(2,1)S(1)}, u32[]{:S(2)}, u32[]{:S(2)}) collective-permute-start(bf16[4,400,128]{2,1,0:T(8,128)(2,1)S(1)} %pad_maximum_fusion.3.refs_0_), channel_id=1, source_target_pairs={{0,2},{1,3},{2,0},{3,1},{4,6},{5,7},{6,4},{7,5},{8,10},{9,11},{10,... | collective-permute-start | bytes 1228808 | tf_op jit(solution)/shard_map/ppermute | solution.py:128
  121.6 18.7 %collective-permute-start.15 = (bf16[4,400,128]{2,1,0:T(8,128)(2,1)S(1)}, bf16[4,400,128]{2,1,0:T(8,128)(2,1)S(1)}, u32[]{:S(2)}, u32[]{:S(2)}) collective-permute-start(bf16[4,400,128]{2,1,0:T(8,128)(2,1)S(1)} %pad_maximum_fusion.4.refs_4_), channel_id=1, source_target_pairs={{0,8},{8,16},{16,24},{24,0},{1,9},{9,17},{17,25},{25,1},{2,10},{10... | collective-permute-start | bytes 1228808 | tf_op jit(solution)/shard_map/ppermute | solution.py:128
  122.0 20.3 %collective-permute-start.16 = (bf16[4,400,128]{2,1,0:T(8,128)(2,1)S(1)}, bf16[4,400,128]{2,1,0:T(8,128)(2,1)S(1)}, u32[]{:S(2)}, u32[]{:S(2)}) collective-permute-start(bf16[4,400,128]{2,1,0:T(8,128)(2,1)S(1)} %pad_maximum_fusion.4.refs_4_), channel_id=1, source_target_pairs={{0,24},{8,0},{16,8},{24,16},{1,25},{9,1},{17,9},{25,17},{2,26},{10... | collective-permute-start | bytes 1228808 | tf_op jit(solution)/shard_map/ppermute | solution.py:128
  124.9 19.0 %collective-permute-start.17 = (bf16[4,400,128]{2,1,0:T(8,128)(2,1)S(1)}, bf16[4,400,128]{2,1,0:T(8,128)(2,1)S(1)}, u32[]{:S(2)}, u32[]{:S(2)}) collective-permute-start(bf16[4,400,128]{2,1,0:T(8,128)(2,1)S(1)} %pad_maximum_fusion.4.refs_4_), channel_id=1, source_target_pairs={{0,16},{8,24},{16,0},{24,8},{1,17},{9,25},{17,1},{25,9},{2,18},{10... | collective-permute-start | bytes 1228808 | tf_op jit(solution)/shard_map/ppermute | solution.py:128
  142.3 0.7 copy-start.2
  143.9 0.7 copy-start.4
  144.6 1.0 copy-start.3
  145.6 1.0 copy-start.5
  155.6 2.0 collective-permute-start.18
  158.2 8.5 %collective-permute-start.19 = (bf16[1,72,512]{2,1,0:T(8,128)(2,1)S(1)}, bf16[1,72,512]{2,1,0:T(8,128)(2,1)S(1)}, u32[]{:S(2)}, u32[]{:S(2)}) collective-permute-start(bf16[1,72,512]{2,1,0:T(8,128)(2,1)S(1)} %get-tuple-element.26), channel_id=1, source_target_pairs={{0,64},{64,128},{128,192},{192,0},{1,65},{65,129},{129,193},{193,1... | collective-permute-start | bytes 221192 | tf_op jit(solution)/shard_map/ppermute | solution.py:241
  163.0 27.2 %copy-start.1 = (f32[2048,512]{1,0:T(8,128)S(1)}, f32[2048,512]{1,0:T(8,128)}, u32[]{:S(2)}) copy-start(f32[2048,512]{1,0:T(8,128)} %basis.3) | copy-start | bytes 12582916
  163.0 6.1 %collective-permute-start.20 = (bf16[1,72,512]{2,1,0:T(8,128)(2,1)S(1)}, bf16[1,72,512]{2,1,0:T(8,128)(2,1)S(1)}, u32[]{:S(2)}, u32[]{:S(2)}) collective-permute-start(bf16[1,72,512]{2,1,0:T(8,128)(2,1)S(1)} %get-tuple-element.28), channel_id=1, source_target_pairs={{0,192},{64,0},{128,64},{192,128},{1,193},{65,1},{129,65},{193,129... | collective-permute-start | bytes 221192 | tf_op jit(solution)/shard_map/ppermute | solution.py:241
  163.0 9.7 %collective-permute-start.21 = (bf16[1,72,512]{2,1,0:T(8,128)(2,1)S(1)}, bf16[1,72,512]{2,1,0:T(8,128)(2,1)S(1)}, u32[]{:S(2)}, u32[]{:S(2)}) collective-permute-start(bf16[1,72,512]{2,1,0:T(8,128)(2,1)S(1)} %get-tuple-element.27), channel_id=1, source_target_pairs={{0,128},{64,192},{128,0},{192,64},{1,129},{65,193},{129,1},{193,65... | collective-permute-start | bytes 221192 | tf_op jit(solution)/shard_map/ppermute | solution.py:241
  187.8 2.0 collective-permute-start.22
  196.2 41.0 %copy-start.9 = (bf16[64,512]{1,0:T(8,128)(2,1)S(1)}, bf16[64,512]{1,0:T(8,128)(2,1)}, u32[]{:S(2)}) copy-start(bf16[64,512]{1,0:T(8,128)(2,1)} %param.12) | copy-start | bytes 196612

commit v3 on v2

--- a/solution.py
+++ b/solution.py
@@ -128,7 +128,14 @@
     return [array] + [lax.ppermute(array, axis, ring(axis, 4 - k)) for k in OFFSETS[1:]]
 
 
-def rotate_in(basis, given, query, out):
+def rotate_in(basis, query_right, train_right, query, out, given):
+    @pl.when(pl.program_id(0) == 0)
+    def _():
+        k, rank = query_right.shape
+        for at in (0, k):
+            given[pl.ds(0, rank), pl.ds(at, k)] = query_right[...].T
+            given[pl.ds(rank, train_right.shape[1]), pl.ds(at, k)] = train_right[...].T
+
     right = jnp.concatenate(halves(basis[...]), axis=0)
     n = given.shape[0] // (2 * SHARE)
     plain = [query[:, k * 128 : (k + 1) * 128] for k in range(query.shape[1] // 128)]
@@ -221,9 +228,11 @@
     return value_of(message[:, :SHARE], jnp.exp2(level)[:, None] * (1.0 / SPAN))
 
 
-def summed_over_chips(array, after):
-    message, _ = lax.optimization_barrier((coded_columns(array, 8), after))
-    arrived = [lax.ppermute(message, "row_0", ring("row_0", step)) for step in (1, 3, 2)]
+def summed_over_chips(array):
+    message = coded_columns(array, 8)
+    arrived = []
+    for step in (2, 3, 1):
+        arrived.append(lax.ppermute(message, "row_0", ring("row_0", step)))
     total = array
     for got in arrived:
         total += column_values(got).reshape(array.shape)
@@ -277,8 +286,6 @@
     n = (rank + train) // 128
     height = n * SHARE + tail_of(n)
     wide = step // 2 * 128
-    given = jnp.concatenate([query_right, train_right], axis=1).T
-    given = jnp.concatenate([given, given], axis=1)
     extra = rank // 128 * SHARE
     message = call(
         rotate_in,
@@ -286,13 +293,20 @@
         cols // step,
         [
             blocks((basis_in.shape[0], wide), 1),
-            whole(given.shape),
+            whole(query_right.shape),
+            whole(train_right.shape),
             whole(query_left.shape),
         ],
         pl.BlockSpec((1, 2, 2, height + extra, 128), lambda i: (i // 2, 0, i % 2, 0, 0)),
-        (pltpu.with_memory_space_constraint(basis_in, pltpu.HBM), given, query_left),
+        (
+            pltpu.with_memory_space_constraint(basis_in, pltpu.HBM),
+            query_right,
+            train_right,
+            query_left,
+        ),
         4 * basis_in.size * (rank + train),
         16,
+        [pltpu.VMEM((rank + train, 2 * basis_in.shape[0]), bf16)],
     ).reshape(cols, height + extra, 128)
     got = exchange(message, COL)
 
@@ -311,7 +325,7 @@
     query = got[:, n * SHARE : n * SHARE + extra].reshape(cols, -1, SHARE, 128)
     query = query.transpose(0, 2, 1, 3).reshape(cols * SHARE, rank)
     rot_left = multiply(high, query, FIRST) + multiply(low, query, FIRST)
-    rot_left = both_halves(summed_over_chips(my_half_summed(rot_left), (firsts, seconds)))
+    rot_left = both_halves(summed_over_chips(my_half_summed(rot_left)))
     high, low = split(rot_left)
     left = jnp.concatenate([high, low, high], axis=1)
 
@@ -332,7 +346,7 @@
             transcendentals=0,
             bytes_accessed=eig_damped.size * 4,
         ),
-        compiler_params=pltpu.CompilerParams(vmem_limit_bytes=18 * 2**20),
+        compiler_params=pltpu.CompilerParams(vmem_limit_bytes=12 * 2**20),
         name="apply_piece",
     )(place, left, pltpu.with_memory_space_constraint(eig_damped, pltpu.HBM), *pieces)
     applied = both_halves(summed_in_turn(my_half_summed(contrib)))

time: 265 us -> 259 us (0.977)
  waiting for transfers between devices: 41.5 us -> 38.7 us
    ppermute x12, waiting for transfers between devices: 21.8 us -> 15.9 us  [around(): lax.ppermute(array, axis, ring(axis, 4 - k))]
    ppermute x3, waiting for transfers between devices: 5.87 us -> 8.85 us  [summed_over_chips(): arrived.append(lax.ppermute(message, 'row_0', ring('row_0', step)))]
    unnamed x26 -> x28, local copies, waits for them, and re-layouts: 7.83 us -> 8.24 us
  transfers between devices with their start and end apart: 23 -> 23, of which waited for: 13 -> 9; matrix products, arithmetic and copies ran while one was open for 2% -> 1% of each run, Pallas kernels for 0% -> 0%
where the time goes in v3:
time: 259 us; the launch traced here: 257 us
  blocking collectives  137 us (53%)
  waiting for transfers between devices  38.7 us (15%)
  starting transfers between devices  35.6 us (14%)
  Pallas kernels  24.1 us (9%)
  local copies, waits for them, and re-layouts  9.54 us (4%)
  other arithmetic  9.17 us (4%)
    all_to_all x4, blocking collectives, exchange(): return lax.all_to_all(pieces, axis, split_axis=0, concat_axis=0, tiled=True)  122 us
    ppermute x12, waiting for transfers between devices, around(): lax.ppermute(array, axis, ring(axis, 4 - k))  15.9 us
    pallas_call x2, Pallas kernels, call(): pl.pallas_call(kernel, out_shape=out, grid=(grid,), in_specs=ins, out_spe...  15.2 us
    ppermute x12, starting transfers between devices, around(): lax.ppermute(array, axis, ring(axis, 4 - k))  14.9 us
    all_gather x1, blocking collectives, summed_in_turn(): lax.all_gather(coded_columns(total, 8), 'row_0', axis=0, tiled=True)  14.6 us
    ppermute x3, starting transfers between devices, summed_over_chips(): arrived.append(lax.ppermute(message, 'row_0', ring('row_0', step)))  11.4 us
    pallas_call x1, Pallas kernels, body(): pl.pallas_call(apply_piece, out_shape=struct((n_out, train), f32), in_spe...  8.9 us
    ppermute x3, waiting for transfers between devices, summed_over_chips(): arrived.append(lax.ppermute(message, 'row_0', ring('row_0', step)))  8.85 us
  transfers between devices with their start and end apart: 23, of which 9 were waited for; matrix products, arithmetic and copies ran while one was open for 1% of the time, Pallas kernels for 0%

profile of v3, /device:TPU:8, one launch (start us, length us, event | category | flops | bytes accessed | tf_op | source)
XLA Modules:
  0.0 257.0 jit_solution(11285513792374623112)
XLA Ops:
  0.6 1.0 copy-done.2
  1.7 0.9 copy-done.7
  2.6 0.8 copy-done.8
  3.4 9.2 %shard_map.86 = bf16[4,2,4,528,128]{4,3,2,1,0:T(8,128)(2,1)S(1)} custom-call(f32[512,2048]{1,0:T(8,128)} %basis.2, bf16[512,256]{1,0:T(8,128)(2,1)S(1)} %copy-done.7, bf16[512,512]{1,0:T(8,128)(2,1)S(1)} %copy-done.2, bf16[64,256]{1,0:T(8,128)(2,1)S(1)} %copy-done.8), custom_call_target="tpu_custom_call" | custom-call | flops 3221225472 | bytes 5013504 | tf_op jit(solution)/shard_map/pallas_call | solution.py:104
  12.6 60.6 %all_to_all.20 = bf16[32,528,128]{2,1,0:T(8,128)(2,1)S(1)} all-to-all(bf16[32,528,128]{2,1,0:T(8,128)(2,1)S(1)} %bitcast.114), channel_id=1, replica_groups=mesh['row_0'=4,'row_1'=2,'col_0'=4,'col_1'=2,'col_2'=4] {'col_0','col_1'..., dimensions={0} | all-to-all | bytes 8650752 | tf_op jit(solution)/shard_map/all_to_all | solution.py:21
  73.2 2.0 copy-done.9
  75.1 2.4 fusion.4
  77.7 0.8 collective-permute-start
  78.5 4.0 %collective-permute-done = bf16[400,128]{1,0:T(8,128)(2,1)S(1)} collective-permute-done((bf16[400,128]{1,0:T(8,128)(2,1)S(1)}, bf16[400,128]{1,0:T(8,128)(2,1)S(1)}, u32[]{:S(2)}, u32[]{:S(2)}) %collective-permute-start) | collective-permute-done | bytes 102432 | tf_op jit(solution)/shard_map/ppermute | solution.py:314
  82.5 1.1 copy.17
  83.6 0.7 fusion.11
  84.4 1.0 fusion.15
  85.4 0.1 collective-permute-start.1
  85.6 0.6 collective-permute-start.9
  86.2 1.4 collective-permute-start.10
  87.6 1.7 collective-permute-start.11
  89.3 0.5 collective-permute-start.6
  89.8 2.8 %collective-permute-start.7 = (bf16[400,128]{1,0:T(8,128)(2,1)S(1)}, bf16[400,128]{1,0:T(8,128)(2,1)S(1)}, u32[]{:S(2)}, u32[]{:S(2)}) collective-permute-start(bf16[400,128]{1,0:T(8,128)(2,1)S(1)} %get-tuple-element.8), channel_id=1, source_target_pairs={{0,24},{8,0},{16,8},{24,16},{1,25},{9,1},{17,9},{25,17},{2,26},{10... | collective-permute-start | bytes 307208 | tf_op jit(solution)/shard_map/ppermute | solution.py:128
  92.7 0.1 fusion.42
  92.8 0.1 maximum_maximum_fusion.1
  93.0 6.5 %collective-permute-start.2 = (bf16[4,72,256]{2,1,0:T(8,128)(2,1)S(1)}, bf16[4,72,256]{2,1,0:T(8,128)(2,1)S(1)}, u32[]{:S(2)}, u32[]{:S(2)}) collective-permute-start(bf16[4,72,256]{2,1,0:T(8,128)(2,1)S(1)} %maximum_maximum_fusion.1), channel_id=1, source_target_pairs={{0,128},{64,192},{128,0},{192,64},{1,129},{65,193},{129,1},{193,65... | collective-permute-start | bytes 442376 | tf_op jit(solution)/shard_map/ppermute | solution.py:235
  99.7 2.7 %collective-permute-start.12 = (bf16[4,400,128]{2,1,0:T(8,128)(2,1)S(1)}, bf16[4,400,128]{2,1,0:T(8,128)(2,1)S(1)}, u32[]{:S(2)}, u32[]{:S(2)}) collective-permute-start(bf16[4,400,128]{2,1,0:T(8,128)(2,1)S(1)} %pad_maximum_fusion.2.refs_0_), channel_id=1, source_target_pairs={{0,1},{1,2},{2,3},{3,0},{4,5},{5,6},{6,7},{7,4},{8,9},{9,10},{10,1... | collective-permute-start | bytes 1228808 | tf_op jit(solution)/shard_map/ppermute | solution.py:128
  102.4 4.9 %collective-permute-start.3 = (bf16[4,72,256]{2,1,0:T(8,128)(2,1)S(1)}, bf16[4,72,256]{2,1,0:T(8,128)(2,1)S(1)}, u32[]{:S(2)}, u32[]{:S(2)}) collective-permute-start(bf16[4,72,256]{2,1,0:T(8,128)(2,1)S(1)} %maximum_maximum_fusion.1), channel_id=1, source_target_pairs={{0,192},{64,0},{128,64},{192,128},{1,193},{65,1},{129,65},{193,129... | collective-permute-start | bytes 442376 | tf_op jit(solution)/shard_map/ppermute | solution.py:235
  107.3 5.1 %collective-permute-done.3 = bf16[4,72,256]{2,1,0:T(8,128)(2,1)S(1)} collective-permute-done((bf16[4,72,256]{2,1,0:T(8,128)(2,1)S(1)}, bf16[4,72,256]{2,1,0:T(8,128)(2,1)S(1)}, u32[]{:S(2)}, u32[]{:S(2)}) %collective-permute-start.3) | collective-permute-done | bytes 147488 | tf_op jit(solution)/shard_map/ppermute | solution.py:235
  112.5 3.7 %collective-permute-done.4 = bf16[4,72,256]{2,1,0:T(8,128)(2,1)S(1)} collective-permute-done((bf16[4,72,256]{2,1,0:T(8,128)(2,1)S(1)}, bf16[4,72,256]{2,1,0:T(8,128)(2,1)S(1)}, u32[]{:S(2)}, u32[]{:S(2)}) %collective-permute-start.4) | collective-permute-done | bytes 147488 | tf_op jit(solution)/shard_map/ppermute | solution.py:235
  116.2 0.1 negate_select_fusion.6
  116.3 0.1 negate_select_fusion.5
  116.4 0.1 negate_select_fusion.4
  116.6 0.1 collective-permute-start.5
  116.8 1.0 collective-permute-start.14
  117.8 0.4 collective-permute-start.15
  118.2 2.8 %collective-permute-start.16 = (bf16[4,400,128]{2,1,0:T(8,128)(2,1)S(1)}, bf16[4,400,128]{2,1,0:T(8,128)(2,1)S(1)}, u32[]{:S(2)}, u32[]{:S(2)}) collective-permute-start(bf16[4,400,128]{2,1,0:T(8,128)(2,1)S(1)} %pad_maximum_fusion.3.refs_4_), channel_id=1, source_target_pairs={{0,24},{8,0},{16,8},{24,16},{1,25},{9,1},{17,9},{25,17},{2,26},{10... | collective-permute-start | bytes 1228808 | tf_op jit(solution)/shard_map/ppermute | solution.py:128
  121.0 0.8 collective-permute-start.17
  121.9 1.3 fusion.25
  123.3 14.1 %collective-permute-done.13.refs_2_ = bf16[4,400,128]{2,1,0:T(8,128)(2,1)S(1)} collective-permute-done((bf16[4,400,128]{2,1,0:T(8,128)(2,1)S(1)}, bf16[4,400,128]{2,1,0:T(8,128)(2,1)S(1)}, u32[]{:S(2)}, u32[]{:S(2)}) %collective-permute-start.13) | collective-permute-done | bytes 409632 | tf_op jit(solution)/shard_map/ppermute | solution.py:128
  137.4 1.8 collective-permute-done.15.refs_5_
  139.2 0.8 copy-done.3
  139.9 0.8 copy-done.5
  140.7 1.0 copy-done.4
  141.7 1.0 copy-done.6
  142.7 8.9 %apply_piece.1 = f32[512,512]{1,0:T(8,128)S(1)} custom-call(s32[2]{0:T(128)S(1)} %pad_add_fusion.place, bf16[512,768]{1,0:T(8,128)(2,1)S(1)} %pad_maximum_fusion.1.left, f32[512,2048]{1,0:T(8,128)} %eig.1, bf16[4,400,128]{2,1,0:T(8,128)(2,1)S(1)} %pad_maximum_fusion.2.refs_0_, bf16[4,400,128]{2,1,0:T(8,128)(2,1)S(1)} %collective-permute-done.12.refs_1_, ...), custom_call_target="tpu_custom_call" | custom-call | flops 4831838208 | bytes 4194304 | tf_op jit(solution)/shard_map/apply_piece/pallas_call | solution.py:333
  151.6 0.1 collective-permute-start.18
  151.8 1.9 collective-permute-done.18
  153.6 0.1 broadcast_compare_fusion
  153.9 0.2 fusion.26
  154.1 0.1 maximum_maximum_fusion
  154.2 2.8 %collective-permute-start.19 = (bf16[1,72,512]{2,1,0:T(8,128)(2,1)S(1)}, bf16[1,72,512]{2,1,0:T(8,128)(2,1)S(1)}, u32[]{:S(2)}, u32[]{:S(2)}) collective-permute-start(bf16[1,72,512]{2,1,0:T(8,128)(2,1)S(1)} %get-tuple-element.24), channel_id=1, source_target_pairs={{0,64},{64,128},{128,192},{192,0},{1,65},{65,129},{129,193},{193,1... | collective-permute-start | bytes 221192 | tf_op jit(solution)/shard_map/ppermute | solution.py:250
  157.0 1.5 collective-permute-start.20
  158.4 4.0 %collective-permute-start.21 = (bf16[1,72,512]{2,1,0:T(8,128)(2,1)S(1)}, bf16[1,72,512]{2,1,0:T(8,128)(2,1)S(1)}, u32[]{:S(2)}, u32[]{:S(2)}) collective-permute-start(bf16[1,72,512]{2,1,0:T(8,128)(2,1)S(1)} %get-tuple-element.25), channel_id=1, source_target_pairs={{0,128},{64,192},{128,0},{192,64},{1,129},{65,193},{129,1},{193,65... | collective-permute-start | bytes 221192 | tf_op jit(solution)/shard_map/ppermute | solution.py:250
  162.4 1.2 collective-permute-done.20
  163.6 5.1 %collective-permute-done.21 = bf16[1,72,512]{2,1,0:T(8,128)(2,1)S(1)} collective-permute-done((bf16[1,72,512]{2,1,0:T(8,128)(2,1)S(1)}, bf16[1,72,512]{2,1,0:T(8,128)(2,1)S(1)}, u32[]{:S(2)}, u32[]{:S(2)}) %collective-permute-start.21) | collective-permute-done | bytes 73760 | tf_op jit(solution)/shard_map/ppermute | solution.py:250
  168.7 0.2 abs_reduce_fusion
  169.0 14.6 %all_gather.3 = bf16[4,72,512]{2,1,0:T(8,128)(2,1)S(1)} all-gather(bf16[1,72,512]{2,1,0:T(8,128)(2,1)S(1)} %maximum_maximum_fusion.2), channel_id=1, replica_groups=mesh['row_0'=4,'row_1'=2,'col_0'=4,'col_1'=2,'col_2'=4] {'row_0'}, dimensions={0}, use_global_device_ids=true | all-gather | bytes 368640 | tf_op jit(solution)/shard_map/all_gather | solution.py:253
  183.7 0.2 negate_select_fusion.2
  184.0 1.9 collective-permute-done.22
  185.9 0.2 reduce-precision_convert_fusion.2
  186.1 0.1 pad_maximum_fusion.given
  186.3 6.0 %shard_map.87 = bf16[32,264,128]{2,1,0:T(8,128)(2,1)S(1)} custom-call(f32[2048,512]{1,0:T(8,128)S(1)} %copy-done.1, bf16[1536,512]{1,0:T(8,128)(2,1)S(1)} %pad_maximum_fusion.given), custom_call_target="tpu_custom_call" | custom-call | flops 3221225472 | bytes 5767168 | tf_op jit(solution)/shard_map/pallas_call | solution.py:104
  192.3 38.5 %all_to_all.21 = bf16[32,264,128]{2,1,0:T(8,128)(2,1)S(1)} all-to-all(bf16[32,264,128]{2,1,0:T(8,128)(2,1)S(1)} %shard_map.87), channel_id=1, replica_groups=mesh['row_0'=4,'row_1'=2,'col_0'=4,'col_1'=2,'col_2'=4] {'col_0','col_1'..., dimensions={0} | all-to-all | bytes 4325376 | tf_op jit(solution)/shard_map/all_to_all | solution.py:21
  230.8 1.5 fusion.10
  232.4 0.7 multiply_reduce_fusion
  233.0 11.8 %all_to_all.22 = f32[32,4,128]{2,1,0:T(4,128)S(1)} all-to-all(f32[32,4,128]{2,1,0:T(4,128)S(1)} %broadcast_in_dim.13), channel_id=1, replica_groups=mesh['row_0'=4,'row_1'=2,'col_0'=4,'col_1'=2,'col_2'=4] {'col_0','col_1'..., dimensions={0} | all-to-all | bytes 131072 | tf_op jit(solution)/shard_map/all_to_all | solution.py:21
  244.9 11.5 %all_to_all.23 = f32[8,4,128]{2,1,0:T(4,128)S(1)} all-to-all(f32[8,4,128]{2,1,0:T(4,128)S(1)} %broadcast_in_dim.14), channel_id=1, replica_groups=mesh['row_0'=4,'row_1'=2,'col_0'=4,'col_1'=2,'col_2'=4] {'row_0','row_1'}, dimensions={0} | all-to-all | bytes 32768 | tf_op jit(solution)/shard_map/all_to_all | solution.py:21
  256.4 0.6 reduce_sum.49
  (80 shorter events, 1.7 us)
Async XLA Ops:
  0.6 1.0 copy-start.2
  1.7 0.9 copy-start.7
  2.6 0.8 copy-start.8
  73.1 2.0 copy-start.9
  77.5 5.0 %slice-start = ((bf16[32,528,128]{2,1,0:T(8,128)(2,1)}), bf16[32,128,128]{2,1,0:T(8,128)(2,1)S(1)}, s32[]{:S(2)}) async-start(bf16[32,528,128]{2,1,0:T(8,128)(2,1)} %copy-done.9), calls=%async_computation.4 | async-start | bytes 2097152 | tf_op jit(solution)/shard_map/slice | solution.py:325
  77.7 4.7 %collective-permute-start = (bf16[400,128]{1,0:T(8,128)(2,1)S(1)}, bf16[400,128]{1,0:T(8,128)(2,1)S(1)}, u32[]{:S(2)}, u32[]{:S(2)}) collective-permute-start(bf16[400,128]{1,0:T(8,128)(2,1)S(1)} %fusion.73), channel_id=1, source_target_pairs={{0,4},{4,0},{1,5},{5,1},{2,6},{6,2},{3,7},{7,3},{8,12},{12,8},{9,1... | collective-permute-start | bytes 307208 | tf_op jit(solution)/shard_map/ppermute | solution.py:314
  78.5 5.1 %copy-start = (f32[2048,512]{1,0:T(8,128)S(1)}, f32[2048,512]{1,0:T(8,128)}, u32[]{:S(2)}) copy-start(f32[2048,512]{1,0:T(8,128)} %basis.3) | copy-start | bytes 12582916
  85.4 4.4 %collective-permute-start.1 = (f32[256,256]{1,0:T(8,128)S(1)}, f32[256,256]{1,0:T(8,128)S(1)}, u32[]{:S(2)}, u32[]{:S(2)}) collective-permute-start(f32[256,256]{1,0:T(8,128)S(1)} %constant_dynamic-slice_fusion.4), channel_id=1, source_target_pairs={{0,32},{32,0},{1,33},{33,1},{2,34},{34,2},{3,35},{35,3},{4,36},{36... | collective-permute-start | bytes 786440 | tf_op jit(solution)/shard_map/ppermute | solution.py:206
  85.6 7.3 %collective-permute-start.9 = (bf16[400,128]{1,0:T(8,128)(2,1)S(1)}, bf16[400,128]{1,0:T(8,128)(2,1)S(1)}, u32[]{:S(2)}, u32[]{:S(2)}) collective-permute-start(bf16[400,128]{1,0:T(8,128)(2,1)S(1)} %get-tuple-element.9), channel_id=1, source_target_pairs={{0,1},{1,2},{2,3},{3,0},{4,5},{5,6},{6,7},{7,4},{8,9},{9,10},{10,1... | collective-permute-start | bytes 307208 | tf_op jit(solution)/shard_map/ppermute | solution.py:128
  86.2 6.8 %collective-permute-start.10 = (bf16[400,128]{1,0:T(8,128)(2,1)S(1)}, bf16[400,128]{1,0:T(8,128)(2,1)S(1)}, u32[]{:S(2)}, u32[]{:S(2)}) collective-permute-start(bf16[400,128]{1,0:T(8,128)(2,1)S(1)} %get-tuple-element.9), channel_id=1, source_target_pairs={{0,3},{1,0},{2,1},{3,2},{4,7},{5,4},{6,5},{7,6},{8,11},{9,8},{10,9... | collective-permute-start | bytes 307208 | tf_op jit(solution)/shard_map/ppermute | solution.py:128
  87.6 11.9 %collective-permute-start.11 = (bf16[400,128]{1,0:T(8,128)(2,1)S(1)}, bf16[400,128]{1,0:T(8,128)(2,1)S(1)}, u32[]{:S(2)}, u32[]{:S(2)}) collective-permute-start(bf16[400,128]{1,0:T(8,128)(2,1)S(1)} %get-tuple-element.9), channel_id=1, source_target_pairs={{0,2},{1,3},{2,0},{3,1},{4,6},{5,7},{6,4},{7,5},{8,10},{9,11},{10,... | collective-permute-start | bytes 307208 | tf_op jit(solution)/shard_map/ppermute | solution.py:128
  89.3 10.3 %collective-permute-start.6 = (bf16[400,128]{1,0:T(8,128)(2,1)S(1)}, bf16[400,128]{1,0:T(8,128)(2,1)S(1)}, u32[]{:S(2)}, u32[]{:S(2)}) collective-permute-start(bf16[400,128]{1,0:T(8,128)(2,1)S(1)} %get-tuple-element.8), channel_id=1, source_target_pairs={{0,8},{8,16},{16,24},{24,0},{1,9},{9,17},{17,25},{25,1},{2,10},{10... | collective-permute-start | bytes 307208 | tf_op jit(solution)/shard_map/ppermute | solution.py:128
  89.8 9.8 %collective-permute-start.7 = (bf16[400,128]{1,0:T(8,128)(2,1)S(1)}, bf16[400,128]{1,0:T(8,128)(2,1)S(1)}, u32[]{:S(2)}, u32[]{:S(2)}) collective-permute-start(bf16[400,128]{1,0:T(8,128)(2,1)S(1)} %get-tuple-element.8), channel_id=1, source_target_pairs={{0,24},{8,0},{16,8},{24,16},{1,25},{9,1},{17,9},{25,17},{2,26},{10... | collective-permute-start | bytes 307208 | tf_op jit(solution)/shard_map/ppermute | solution.py:128
  92.9 6.7 %collective-permute-start.8 = (bf16[400,128]{1,0:T(8,128)(2,1)S(1)}, bf16[400,128]{1,0:T(8,128)(2,1)S(1)}, u32[]{:S(2)}, u32[]{:S(2)}) collective-permute-start(bf16[400,128]{1,0:T(8,128)(2,1)S(1)} %get-tuple-element.8), channel_id=1, source_target_pairs={{0,16},{8,24},{16,0},{24,8},{1,17},{9,25},{17,1},{25,9},{2,18},{10... | collective-permute-start | bytes 307208 | tf_op jit(solution)/shard_map/ppermute | solution.py:128
  93.0 14.3 %collective-permute-start.2 = (bf16[4,72,256]{2,1,0:T(8,128)(2,1)S(1)}, bf16[4,72,256]{2,1,0:T(8,128)(2,1)S(1)}, u32[]{:S(2)}, u32[]{:S(2)}) collective-permute-start(bf16[4,72,256]{2,1,0:T(8,128)(2,1)S(1)} %maximum_maximum_fusion.1), channel_id=1, source_target_pairs={{0,128},{64,192},{128,0},{192,64},{1,129},{65,193},{129,1},{193,65... | collective-permute-start | bytes 442376 | tf_op jit(solution)/shard_map/ppermute | solution.py:235
  99.7 18.6 %collective-permute-start.12 = (bf16[4,400,128]{2,1,0:T(8,128)(2,1)S(1)}, bf16[4,400,128]{2,1,0:T(8,128)(2,1)S(1)}, u32[]{:S(2)}, u32[]{:S(2)}) collective-permute-start(bf16[4,400,128]{2,1,0:T(8,128)(2,1)S(1)} %pad_maximum_fusion.2.refs_0_), channel_id=1, source_target_pairs={{0,1},{1,2},{2,3},{3,0},{4,5},{5,6},{6,7},{7,4},{8,9},{9,10},{10,1... | collective-permute-start | bytes 1228808 | tf_op jit(solution)/shard_map/ppermute | solution.py:128
  102.4 10.1 %collective-permute-start.3 = (bf16[4,72,256]{2,1,0:T(8,128)(2,1)S(1)}, bf16[4,72,256]{2,1,0:T(8,128)(2,1)S(1)}, u32[]{:S(2)}, u32[]{:S(2)}) collective-permute-start(bf16[4,72,256]{2,1,0:T(8,128)(2,1)S(1)} %maximum_maximum_fusion.1), channel_id=1, source_target_pairs={{0,192},{64,0},{128,64},{192,128},{1,193},{65,1},{129,65},{193,129... | collective-permute-start | bytes 442376 | tf_op jit(solution)/shard_map/ppermute | solution.py:235
  107.3 8.9 %collective-permute-start.4 = (bf16[4,72,256]{2,1,0:T(8,128)(2,1)S(1)}, bf16[4,72,256]{2,1,0:T(8,128)(2,1)S(1)}, u32[]{:S(2)}, u32[]{:S(2)}) collective-permute-start(bf16[4,72,256]{2,1,0:T(8,128)(2,1)S(1)} %maximum_maximum_fusion.1), channel_id=1, source_target_pairs={{0,64},{64,128},{128,192},{192,0},{1,65},{65,129},{129,193},{193,1... | collective-permute-start | bytes 442376 | tf_op jit(solution)/shard_map/ppermute | solution.py:235
  116.6 4.4 %copy-start.10 = (f32[256,256]{1,0:T(8,128)}, f32[256,256]{1,0:T(8,128)S(1)}, u32[]{:S(2)}) copy-start(f32[256,256]{1,0:T(8,128)S(1)} %bitcast_add_fusion) | copy-start | bytes 786436
  116.6 4.4 %collective-permute-start.5 = (f32[256,256]{1,0:T(8,128)S(1)}, f32[256,256]{1,0:T(8,128)}, u32[]{:S(2)}, u32[]{:S(2)}) collective-permute-start(f32[256,256]{1,0:T(8,128)S(1)} %bitcast_add_fusion), channel_id=1, source_target_pairs={{0,32},{32,0},{1,33},{33,1},{2,34},{34,2},{3,35},{35,3},{4,36},{36... | collective-permute-start | bytes 786440 | tf_op jit(solution)/shard_map/ppermute | solution.py:211
  116.7 20.6 %collective-permute-start.13 = (bf16[4,400,128]{2,1,0:T(8,128)(2,1)S(1)}, bf16[4,400,128]{2,1,0:T(8,128)(2,1)S(1)}, u32[]{:S(2)}, u32[]{:S(2)}) collective-permute-start(bf16[4,400,128]{2,1,0:T(8,128)(2,1)S(1)} %pad_maximum_fusion.2.refs_0_), channel_id=1, source_target_pairs={{0,3},{1,0},{2,1},{3,2},{4,7},{5,4},{6,5},{7,6},{8,11},{9,8},{10,9... | collective-permute-start | bytes 1228808 | tf_op jit(solution)/shard_map/ppermute | solution.py:128
  116.8 20.6 %collective-permute-start.14 = (bf16[4,400,128]{2,1,0:T(8,128)(2,1)S(1)}, bf16[4,400,128]{2,1,0:T(8,128)(2,1)S(1)}, u32[]{:S(2)}, u32[]{:S(2)}) collective-permute-start(bf16[4,400,128]{2,1,0:T(8,128)(2,1)S(1)} %pad_maximum_fusion.2.refs_0_), channel_id=1, source_target_pairs={{0,2},{1,3},{2,0},{3,1},{4,6},{5,7},{6,4},{7,5},{8,10},{9,11},{10,... | collective-permute-start | bytes 1228808 | tf_op jit(solution)/shard_map/ppermute | solution.py:128
  117.8 21.4 %collective-permute-start.15 = (bf16[4,400,128]{2,1,0:T(8,128)(2,1)S(1)}, bf16[4,400,128]{2,1,0:T(8,128)(2,1)S(1)}, u32[]{:S(2)}, u32[]{:S(2)}) collective-permute-start(bf16[4,400,128]{2,1,0:T(8,128)(2,1)S(1)} %pad_maximum_fusion.3.refs_4_), channel_id=1, source_target_pairs={{0,8},{8,16},{16,24},{24,0},{1,9},{9,17},{17,25},{25,1},{2,10},{10... | collective-permute-start | bytes 1228808 | tf_op jit(solution)/shard_map/ppermute | solution.py:128
  118.2 20.9 %collective-permute-start.16 = (bf16[4,400,128]{2,1,0:T(8,128)(2,1)S(1)}, bf16[4,400,128]{2,1,0:T(8,128)(2,1)S(1)}, u32[]{:S(2)}, u32[]{:S(2)}) collective-permute-start(bf16[4,400,128]{2,1,0:T(8,128)(2,1)S(1)} %pad_maximum_fusion.3.refs_4_), channel_id=1, source_target_pairs={{0,24},{8,0},{16,8},{24,16},{1,25},{9,1},{17,9},{25,17},{2,26},{10... | collective-permute-start | bytes 1228808 | tf_op jit(solution)/shard_map/ppermute | solution.py:128
  121.0 18.9 %collective-permute-start.17 = (bf16[4,400,128]{2,1,0:T(8,128)(2,1)S(1)}, bf16[4,400,128]{2,1,0:T(8,128)(2,1)S(1)}, u32[]{:S(2)}, u32[]{:S(2)}) collective-permute-start(bf16[4,400,128]{2,1,0:T(8,128)(2,1)S(1)} %pad_maximum_fusion.3.refs_4_), channel_id=1, source_target_pairs={{0,16},{8,24},{16,0},{24,8},{1,17},{9,25},{17,1},{25,9},{2,18},{10... | collective-permute-start | bytes 1228808 | tf_op jit(solution)/shard_map/ppermute | solution.py:128
  139.2 0.8 copy-start.3
  139.9 0.8 copy-start.5
  140.7 1.0 copy-start.4
  141.7 1.0 copy-start.6
  151.6 2.0 collective-permute-start.18
  154.2 8.2 %collective-permute-start.19 = (bf16[1,72,512]{2,1,0:T(8,128)(2,1)S(1)}, bf16[1,72,512]{2,1,0:T(8,128)(2,1)S(1)}, u32[]{:S(2)}, u32[]{:S(2)}) collective-permute-start(bf16[1,72,512]{2,1,0:T(8,128)(2,1)S(1)} %get-tuple-element.24), channel_id=1, source_target_pairs={{0,64},{64,128},{128,192},{192,0},{1,65},{65,129},{129,193},{193,1... | collective-permute-start | bytes 221192 | tf_op jit(solution)/shard_map/ppermute | solution.py:250
  157.0 29.3 %copy-start.1 = (f32[2048,512]{1,0:T(8,128)S(1)}, f32[2048,512]{1,0:T(8,128)}, u32[]{:S(2)}) copy-start(f32[2048,512]{1,0:T(8,128)} %basis.3) | copy-start | bytes 12582916
  157.0 6.6 %collective-permute-start.20 = (bf16[1,72,512]{2,1,0:T(8,128)(2,1)S(1)}, bf16[1,72,512]{2,1,0:T(8,128)(2,1)S(1)}, u32[]{:S(2)}, u32[]{:S(2)}) collective-permute-start(bf16[1,72,512]{2,1,0:T(8,128)(2,1)S(1)} %get-tuple-element.26), channel_id=1, source_target_pairs={{0,192},{64,0},{128,64},{192,128},{1,193},{65,1},{129,65},{193,129... | collective-permute-start | bytes 221192 | tf_op jit(solution)/shard_map/ppermute | solution.py:250
  158.4 10.2 %collective-permute-start.21 = (bf16[1,72,512]{2,1,0:T(8,128)(2,1)S(1)}, bf16[1,72,512]{2,1,0:T(8,128)(2,1)S(1)}, u32[]{:S(2)}, u32[]{:S(2)}) collective-permute-start(bf16[1,72,512]{2,1,0:T(8,128)(2,1)S(1)} %get-tuple-element.25), channel_id=1, source_target_pairs={{0,128},{64,192},{128,0},{192,64},{1,129},{65,193},{129,1},{193,65... | collective-permute-start | bytes 221192 | tf_op jit(solution)/shard_map/ppermute | solution.py:250
  183.9 2.0 collective-permute-start.22
  192.3 40.1 %copy-start.11 = (bf16[64,512]{1,0:T(8,128)(2,1)S(1)}, bf16[64,512]{1,0:T(8,128)(2,1)}, u32[]{:S(2)}) copy-start(bf16[64,512]{1,0:T(8,128)(2,1)} %param.12) | copy-start | bytes 196612

commit v4 on v3

--- a/solution.py
+++ b/solution.py
@@ -198,16 +198,14 @@
         put_blocks(out, d, [partial[rows, k * 128 : (k + 1) * 128] for k in range(n)])
 
 
-def my_half_summed(array):
-    core = lax.axis_index("row_1")
+def my_half_summed(array, core):
     rows = array.shape[0] // 2
     mine = lax.dynamic_slice_in_dim(array, core * rows, rows, 0)
     other = lax.dynamic_slice_in_dim(array, (1 - core) * rows, rows, 0)
     return mine + lax.ppermute(other, "row_1", ring("row_1", 1))
 
 
-def both_halves(half):
-    core = lax.axis_index("row_1")
+def both_halves(half, core):
     other = lax.ppermute(half, "row_1", ring("row_1", 1))
     return jnp.where(
         core == 0, jnp.concatenate([half, other], 0), jnp.concatenate([other, half], 0)
@@ -245,7 +243,7 @@
     message = coded_columns(array, 8)
     total = lax.dynamic_slice_in_dim(array, me * SHARE, SHARE, 0)
     arrived = []
-    for step in (1, 3, 2):
+    for step in (2, 3, 1):
         piece = lax.dynamic_index_in_dim(message, lax.rem(me + step, chips), 0)
         arrived.append(lax.ppermute(piece, "row_0", ring("row_0", step)))
     for got in arrived:
@@ -281,6 +279,7 @@
     rank, train = query_right.shape[1], train_right.shape[1]
     n_out, _ = eig_damped.shape
     struct = jax.ShapeDtypeStruct
+    core, query_left = lax.optimization_barrier((lax.axis_index("row_1"), query_left))
 
     step = 4
     n = (rank + train) // 128
@@ -308,14 +307,13 @@
         16,
         [pltpu.VMEM((rank + train, 2 * basis_in.shape[0]), bf16)],
     ).reshape(cols, height + extra, 128)
-    got = exchange(message, COL)
-
-    message = message_of(sum_of(got, n))
+    core, got = lax.optimization_barrier((core, exchange(message, COL)))
+
+    message, got = lax.optimization_barrier((message_of(sum_of(got, n)), got))
     other = lax.ppermute(message, "col_1", ring("col_1", 1))
     is_first = lax.axis_index("col_1") == 0
     first = jnp.where(is_first, message, other)
     second = jnp.where(is_first, other, message)
-    first, second, got = lax.optimization_barrier((first, second, got))
     firsts = jnp.stack(around(first, "col_0"))
     seconds = jnp.stack(around(second, "col_2"))
     firsts, seconds = lax.optimization_barrier((firsts, seconds))
@@ -325,7 +323,7 @@
     query = got[:, n * SHARE : n * SHARE + extra].reshape(cols, -1, SHARE, 128)
     query = query.transpose(0, 2, 1, 3).reshape(cols * SHARE, rank)
     rot_left = multiply(high, query, FIRST) + multiply(low, query, FIRST)
-    rot_left = both_halves(summed_over_chips(my_half_summed(rot_left)))
+    rot_left = both_halves(summed_over_chips(my_half_summed(rot_left, core)), core)
     high, low = split(rot_left)
     left = jnp.concatenate([high, low, high], axis=1)
 
@@ -349,7 +347,7 @@
         compiler_params=pltpu.CompilerParams(vmem_limit_bytes=12 * 2**20),
         name="apply_piece",
     )(place, left, pltpu.with_memory_space_constraint(eig_damped, pltpu.HBM), *pieces)
-    applied = both_halves(summed_in_turn(my_half_summed(contrib)))
+    applied = both_halves(summed_in_turn(my_half_summed(contrib, core)), core)
     response = jnp.concatenate(respond_to(basis_out, applied), axis=1)
     scores = jnp.sum(train_left.astype(f32) * response, axis=0).reshape(-1, 128)
     scores = jnp.sum(to_everyone(scores, COL), axis=0)

time: 259 us -> 256 us (0.988)
  waiting for transfers between devices: 38.7 us -> 35.3 us
    ppermute x1, waiting for transfers between devices: 3.96 us -> 0.01 us  [body(): other = lax.ppermute(message, 'col_1', ring('col_1', 1))]
  transfers between devices with their start and end apart: 23 -> 23, of which waited for: 9 -> 9; matrix products, arithmetic and copies ran while one was open for 1% -> 3% of each run, Pallas kernels for 0% -> 0%
where the time goes in v4:
time: 256 us; the launch traced here: 254 us
  blocking collectives  137 us (54%)
  waiting for transfers between devices  35.3 us (14%)
  starting transfers between devices  34.3 us (13%)
  Pallas kernels  24 us (9%)
  local copies, waits for them, and re-layouts  11.2 us (4%)
  other arithmetic  9.21 us (4%)
    all_to_all x4, blocking collectives, exchange(): return lax.all_to_all(pieces, axis, split_axis=0, concat_axis=0, tiled=True)  121 us
    ppermute x12, waiting for transfers between devices, around(): lax.ppermute(array, axis, ring(axis, 4 - k))  15.8 us
    ppermute x12, starting transfers between devices, around(): lax.ppermute(array, axis, ring(axis, 4 - k))  15.6 us
    all_gather x1, blocking collectives, summed_in_turn(): lax.all_gather(coded_columns(total, 8), 'row_0', axis=0, tiled=True)  15.4 us
    pallas_call x2, Pallas kernels, call(): pl.pallas_call(kernel, out_shape=out, grid=(grid,), in_specs=ins, out_spe...  15.2 us
    ppermute x3, starting transfers between devices, summed_over_chips(): arrived.append(lax.ppermute(message, 'row_0', ring('row_0', step)))  11.5 us
    pallas_call x1, Pallas kernels, body(): pl.pallas_call(apply_piece, out_shape=struct((n_out, train), f32), in_spe...  8.82 us
    ppermute x3, waiting for transfers between devices, summed_over_chips(): arrived.append(lax.ppermute(message, 'row_0', ring('row_0', step)))  8.65 us
  transfers between devices with their start and end apart: 23, of which 9 were waited for; matrix products, arithmetic and copies ran while one was open for 3% of the time, Pallas kernels for 0%

profile of v4, /device:TPU:8, one launch (start us, length us, event | category | flops | bytes accessed | tf_op | source)
XLA Modules:
  0.0 253.6 jit_solution(11389661523430148361)
XLA Ops:
  0.6 1.0 copy-done.2
  1.7 0.9 copy-done.7
  2.6 0.8 copy-done.8
  3.4 9.2 %shard_map.86 = bf16[4,2,4,528,128]{4,3,2,1,0:T(8,128)(2,1)S(1)} custom-call(f32[512,2048]{1,0:T(8,128)} %basis.2, bf16[512,256]{1,0:T(8,128)(2,1)S(1)} %copy-done.7, bf16[512,512]{1,0:T(8,128)(2,1)S(1)} %copy-done.2, bf16[64,256]{1,0:T(8,128)(2,1)S(1)} %copy-done.8), custom_call_target="tpu_custom_call" | custom-call | flops 3221225472 | bytes 5013504 | tf_op jit(solution)/shard_map/pallas_call | solution.py:104
  12.6 60.5 %all_to_all.20 = bf16[32,528,128]{2,1,0:T(8,128)(2,1)S(1)} all-to-all(bf16[32,528,128]{2,1,0:T(8,128)(2,1)S(1)} %bitcast.114), channel_id=1, replica_groups=mesh['row_0'=4,'row_1'=2,'col_0'=4,'col_1'=2,'col_2'=4] {'col_0','col_1'..., dimensions={0} | all-to-all | bytes 8650752 | tf_op jit(solution)/shard_map/all_to_all | solution.py:21
  73.2 2.0 copy-done.9
  75.1 2.4 fusion.4
  77.7 0.8 collective-permute-start.5
  78.5 1.6 slice.103
  80.2 1.1 copy.17
  81.3 0.7 fusion.11
  82.0 1.0 fusion.15
  83.0 0.1 collective-permute-start
  83.3 2.0 collective-permute-start.10
  85.3 1.5 collective-permute-start.11
  86.8 0.5 collective-permute-start.6
  87.3 2.7 %collective-permute-start.7 = (bf16[400,128]{1,0:T(8,128)(2,1)S(1)}, bf16[400,128]{1,0:T(8,128)(2,1)S(1)}, u32[]{:S(2)}, u32[]{:S(2)}) collective-permute-start(bf16[400,128]{1,0:T(8,128)(2,1)S(1)} %get-tuple-element.34), channel_id=1, source_target_pairs={{0,24},{8,0},{16,8},{24,16},{1,25},{9,1},{17,9},{25,17},{2,26},{10... | collective-permute-start | bytes 307208 | tf_op jit(solution)/shard_map/ppermute | solution.py:128
  90.2 0.1 fusion.42
  90.3 0.1 maximum_maximum_fusion.1
  90.4 0.1 collective-permute-start.8
  90.5 6.6 %collective-permute-start.1 = (bf16[4,72,256]{2,1,0:T(8,128)(2,1)S(1)}, bf16[4,72,256]{2,1,0:T(8,128)(2,1)S(1)}, u32[]{:S(2)}, u32[]{:S(2)}) collective-permute-start(bf16[4,72,256]{2,1,0:T(8,128)(2,1)S(1)} %maximum_maximum_fusion.1), channel_id=1, source_target_pairs={{0,128},{64,192},{128,0},{192,64},{1,129},{65,193},{129,1},{193,65... | collective-permute-start | bytes 442376 | tf_op jit(solution)/shard_map/ppermute | solution.py:233
  97.2 2.7 %collective-permute-start.12 = (bf16[4,400,128]{2,1,0:T(8,128)(2,1)S(1)}, bf16[4,400,128]{2,1,0:T(8,128)(2,1)S(1)}, u32[]{:S(2)}, u32[]{:S(2)}) collective-permute-start(bf16[4,400,128]{2,1,0:T(8,128)(2,1)S(1)} %pad_maximum_fusion.2.refs_0_), channel_id=1, source_target_pairs={{0,1},{1,2},{2,3},{3,0},{4,5},{5,6},{6,7},{7,4},{8,9},{9,10},{10,1... | collective-permute-start | bytes 1228808 | tf_op jit(solution)/shard_map/ppermute | solution.py:128
  99.9 4.9 %collective-permute-start.2 = (bf16[4,72,256]{2,1,0:T(8,128)(2,1)S(1)}, bf16[4,72,256]{2,1,0:T(8,128)(2,1)S(1)}, u32[]{:S(2)}, u32[]{:S(2)}) collective-permute-start(bf16[4,72,256]{2,1,0:T(8,128)(2,1)S(1)} %maximum_maximum_fusion.1), channel_id=1, source_target_pairs={{0,192},{64,0},{128,64},{192,128},{1,193},{65,1},{129,65},{193,129... | collective-permute-start | bytes 442376 | tf_op jit(solution)/shard_map/ppermute | solution.py:233
  104.8 5.9 %collective-permute-done.2 = bf16[4,72,256]{2,1,0:T(8,128)(2,1)S(1)} collective-permute-done((bf16[4,72,256]{2,1,0:T(8,128)(2,1)S(1)}, bf16[4,72,256]{2,1,0:T(8,128)(2,1)S(1)}, u32[]{:S(2)}, u32[]{:S(2)}) %collective-permute-start.2) | collective-permute-done | bytes 147488 | tf_op jit(solution)/shard_map/ppermute | solution.py:233
  110.7 2.8 %collective-permute-done.3 = bf16[4,72,256]{2,1,0:T(8,128)(2,1)S(1)} collective-permute-done((bf16[4,72,256]{2,1,0:T(8,128)(2,1)S(1)}, bf16[4,72,256]{2,1,0:T(8,128)(2,1)S(1)}, u32[]{:S(2)}, u32[]{:S(2)}) %collective-permute-start.3) | collective-permute-done | bytes 147488 | tf_op jit(solution)/shard_map/ppermute | solution.py:233
  113.6 0.1 negate_select_fusion.6
  113.7 0.1 negate_select_fusion.5
  113.8 0.1 negate_select_fusion.4
  114.0 0.1 collective-permute-start.4
  114.1 1.9 collective-permute-start.14
  116.0 0.5 collective-permute-start.15
  116.5 2.8 %collective-permute-start.16 = (bf16[4,400,128]{2,1,0:T(8,128)(2,1)S(1)}, bf16[4,400,128]{2,1,0:T(8,128)(2,1)S(1)}, u32[]{:S(2)}, u32[]{:S(2)}) collective-permute-start(bf16[4,400,128]{2,1,0:T(8,128)(2,1)S(1)} %pad_maximum_fusion.3.refs_4_), channel_id=1, source_target_pairs={{0,24},{8,0},{16,8},{24,16},{1,25},{9,1},{17,9},{25,17},{2,26},{10... | collective-permute-start | bytes 1228808 | tf_op jit(solution)/shard_map/ppermute | solution.py:128
  119.3 0.9 collective-permute-start.17
  120.2 1.3 fusion.25
  121.6 4.6 %collective-permute-done.13.refs_2_ = bf16[4,400,128]{2,1,0:T(8,128)(2,1)S(1)} collective-permute-done((bf16[4,400,128]{2,1,0:T(8,128)(2,1)S(1)}, bf16[4,400,128]{2,1,0:T(8,128)(2,1)S(1)}, u32[]{:S(2)}, u32[]{:S(2)}) %collective-permute-start.13) | collective-permute-done | bytes 409632 | tf_op jit(solution)/shard_map/ppermute | solution.py:128
  126.2 8.6 %collective-permute-done.14.refs_3_ = bf16[4,400,128]{2,1,0:T(8,128)(2,1)S(1)} collective-permute-done((bf16[4,400,128]{2,1,0:T(8,128)(2,1)S(1)}, bf16[4,400,128]{2,1,0:T(8,128)(2,1)S(1)}, u32[]{:S(2)}, u32[]{:S(2)}) %collective-permute-start.14) | collective-permute-done | bytes 409632 | tf_op jit(solution)/shard_map/ppermute | solution.py:128
  134.7 2.7 %collective-permute-done.15.refs_5_ = bf16[4,400,128]{2,1,0:T(8,128)(2,1)S(1)} collective-permute-done((bf16[4,400,128]{2,1,0:T(8,128)(2,1)S(1)}, bf16[4,400,128]{2,1,0:T(8,128)(2,1)S(1)}, u32[]{:S(2)}, u32[]{:S(2)}) %collective-permute-start.15) | collective-permute-done | bytes 409632 | tf_op jit(solution)/shard_map/ppermute | solution.py:128
  137.4 0.7 copy-done.3
  138.2 0.7 copy-done.5
  138.9 1.0 copy-done.4
  139.9 1.0 copy-done.6
  140.9 8.8 %apply_piece.1 = f32[512,512]{1,0:T(8,128)S(1)} custom-call(s32[2]{0:T(128)S(1)} %pad_add_fusion.place, bf16[512,768]{1,0:T(8,128)(2,1)S(1)} %pad_maximum_fusion.1.left, f32[512,2048]{1,0:T(8,128)} %eig.1, bf16[4,400,128]{2,1,0:T(8,128)(2,1)S(1)} %pad_maximum_fusion.2.refs_0_, bf16[4,400,128]{2,1,0:T(8,128)(2,1)S(1)} %collective-permute-done.12.refs_1_, ...), custom_call_target="tpu_custom_call" | custom-call | flops 4831838208 | bytes 4194304 | tf_op jit(solution)/shard_map/apply_piece/pallas_call | solution.py:331
  149.9 1.9 collective-permute-done.18
  151.8 0.1 broadcast_compare_fusion
  152.0 0.2 fusion.26
  152.2 0.1 maximum_maximum_fusion
  152.4 2.7 %collective-permute-start.19 = (bf16[1,72,512]{2,1,0:T(8,128)(2,1)S(1)}, bf16[1,72,512]{2,1,0:T(8,128)(2,1)S(1)}, u32[]{:S(2)}, u32[]{:S(2)}) collective-permute-start(bf16[1,72,512]{2,1,0:T(8,128)(2,1)S(1)} %get-tuple-element.30), channel_id=1, source_target_pairs={{0,128},{64,192},{128,0},{192,64},{1,129},{65,193},{129,1},{193,65... | collective-permute-start | bytes 221192 | tf_op jit(solution)/shard_map/ppermute | solution.py:248
  155.0 2.9 %collective-permute-start.20 = (bf16[1,72,512]{2,1,0:T(8,128)(2,1)S(1)}, bf16[1,72,512]{2,1,0:T(8,128)(2,1)S(1)}, u32[]{:S(2)}, u32[]{:S(2)}) collective-permute-start(bf16[1,72,512]{2,1,0:T(8,128)(2,1)S(1)} %get-tuple-element.32), channel_id=1, source_target_pairs={{0,192},{64,0},{128,64},{192,128},{1,193},{65,1},{129,65},{193,129... | collective-permute-start | bytes 221192 | tf_op jit(solution)/shard_map/ppermute | solution.py:248
  158.0 0.4 collective-permute-start.21
  158.4 2.4 collective-permute-done.19
  160.8 4.7 %collective-permute-done.20 = bf16[1,72,512]{2,1,0:T(8,128)(2,1)S(1)} collective-permute-done((bf16[1,72,512]{2,1,0:T(8,128)(2,1)S(1)}, bf16[1,72,512]{2,1,0:T(8,128)(2,1)S(1)}, u32[]{:S(2)}, u32[]{:S(2)}) %collective-permute-start.20) | collective-permute-done | bytes 73760 | tf_op jit(solution)/shard_map/ppermute | solution.py:248
  165.5 0.2 abs_reduce_fusion
  165.9 15.4 %all_gather.3 = bf16[4,72,512]{2,1,0:T(8,128)(2,1)S(1)} all-gather(bf16[1,72,512]{2,1,0:T(8,128)(2,1)S(1)} %maximum_maximum_fusion.2), channel_id=1, replica_groups=mesh['row_0'=4,'row_1'=2,'col_0'=4,'col_1'=2,'col_2'=4] {'row_0'}, dimensions={0}, use_global_device_ids=true | all-gather | bytes 368640 | tf_op jit(solution)/shard_map/all_gather | solution.py:251
  181.3 0.2 negate_select_fusion.2
  181.5 1.9 collective-permute-done.22
  183.4 0.2 reduce-precision_convert_fusion.2
  183.7 0.1 pad_maximum_fusion.given
  183.8 6.0 %shard_map.87 = bf16[32,264,128]{2,1,0:T(8,128)(2,1)S(1)} custom-call(f32[2048,512]{1,0:T(8,128)S(1)} %copy-done.1, bf16[1536,512]{1,0:T(8,128)(2,1)S(1)} %pad_maximum_fusion.given), custom_call_target="tpu_custom_call" | custom-call | flops 3221225472 | bytes 5767168 | tf_op jit(solution)/shard_map/pallas_call | solution.py:104
  189.8 37.2 %all_to_all.21 = bf16[32,264,128]{2,1,0:T(8,128)(2,1)S(1)} all-to-all(bf16[32,264,128]{2,1,0:T(8,128)(2,1)S(1)} %shard_map.87), channel_id=1, replica_groups=mesh['row_0'=4,'row_1'=2,'col_0'=4,'col_1'=2,'col_2'=4] {'col_0','col_1'..., dimensions={0} | all-to-all | bytes 4325376 | tf_op jit(solution)/shard_map/all_to_all | solution.py:21
  227.1 1.5 fusion.10
  228.6 0.7 multiply_reduce_fusion
  229.3 11.8 %all_to_all.22 = f32[32,4,128]{2,1,0:T(4,128)S(1)} all-to-all(f32[32,4,128]{2,1,0:T(4,128)S(1)} %broadcast_in_dim.13), channel_id=1, replica_groups=mesh['row_0'=4,'row_1'=2,'col_0'=4,'col_1'=2,'col_2'=4] {'col_0','col_1'..., dimensions={0} | all-to-all | bytes 131072 | tf_op jit(solution)/shard_map/all_to_all | solution.py:21
  241.2 11.8 %all_to_all.23 = f32[8,4,128]{2,1,0:T(4,128)S(1)} all-to-all(f32[8,4,128]{2,1,0:T(4,128)S(1)} %broadcast_in_dim.14), channel_id=1, replica_groups=mesh['row_0'=4,'row_1'=2,'col_0'=4,'col_1'=2,'col_2'=4] {'row_0','row_1'}, dimensions={0} | all-to-all | bytes 32768 | tf_op jit(solution)/shard_map/all_to_all | solution.py:21
  253.0 0.6 reduce_sum.49
  (79 shorter events, 1.7 us)
Async XLA Ops:
  0.6 1.0 copy-start.2
  1.7 0.9 copy-start.7
  2.6 0.8 copy-start.8
  73.1 2.0 copy-start.9
  77.6 3.7 %copy-start = (f32[2048,512]{1,0:T(8,128)S(1)}, f32[2048,512]{1,0:T(8,128)}, u32[]{:S(2)}) copy-start(f32[2048,512]{1,0:T(8,128)} %basis.3) | copy-start | bytes 12582916
  77.7 5.5 %collective-permute-start.5 = (bf16[400,128]{1,0:T(8,128)(2,1)S(1)}, bf16[400,128]{1,0:T(8,128)(2,1)S(1)}, u32[]{:S(2)}, u32[]{:S(2)}) collective-permute-start(bf16[400,128]{1,0:T(8,128)(2,1)S(1)} %fusion.73), channel_id=1, source_target_pairs={{0,4},{4,0},{1,5},{5,1},{2,6},{6,2},{3,7},{7,3},{8,12},{12,8},{9,1... | collective-permute-start | bytes 307208 | tf_op jit(solution)/shard_map/ppermute | solution.py:313
  83.0 4.3 %collective-permute-start = (f32[256,256]{1,0:T(8,128)S(1)}, f32[256,256]{1,0:T(8,128)S(1)}, u32[]{:S(2)}, u32[]{:S(2)}) collective-permute-start(f32[256,256]{1,0:T(8,128)S(1)} %constant_dynamic-slice_fusion.4), channel_id=1, source_target_pairs={{0,32},{32,0},{1,33},{33,1},{2,34},{34,2},{3,35},{35,3},{4,36},{36... | collective-permute-start | bytes 786440 | tf_op jit(solution)/shard_map/ppermute | solution.py:205
  83.2 7.1 %collective-permute-start.9 = (bf16[400,128]{1,0:T(8,128)(2,1)S(1)}, bf16[400,128]{1,0:T(8,128)(2,1)S(1)}, u32[]{:S(2)}, u32[]{:S(2)}) collective-permute-start(bf16[400,128]{1,0:T(8,128)(2,1)S(1)} %get-tuple-element.33), channel_id=1, source_target_pairs={{0,1},{1,2},{2,3},{3,0},{4,5},{5,6},{6,7},{7,4},{8,9},{9,10},{10,1... | collective-permute-start | bytes 307208 | tf_op jit(solution)/shard_map/ppermute | solution.py:128
  83.3 7.2 %collective-permute-start.10 = (bf16[400,128]{1,0:T(8,128)(2,1)S(1)}, bf16[400,128]{1,0:T(8,128)(2,1)S(1)}, u32[]{:S(2)}, u32[]{:S(2)}) collective-permute-start(bf16[400,128]{1,0:T(8,128)(2,1)S(1)} %get-tuple-element.33), channel_id=1, source_target_pairs={{0,3},{1,0},{2,1},{3,2},{4,7},{5,4},{6,5},{7,6},{8,11},{9,8},{10,9... | collective-permute-start | bytes 307208 | tf_op jit(solution)/shard_map/ppermute | solution.py:128
  85.3 11.7 %collective-permute-start.11 = (bf16[400,128]{1,0:T(8,128)(2,1)S(1)}, bf16[400,128]{1,0:T(8,128)(2,1)S(1)}, u32[]{:S(2)}, u32[]{:S(2)}) collective-permute-start(bf16[400,128]{1,0:T(8,128)(2,1)S(1)} %get-tuple-element.33), channel_id=1, source_target_pairs={{0,2},{1,3},{2,0},{3,1},{4,6},{5,7},{6,4},{7,5},{8,10},{9,11},{10,... | collective-permute-start | bytes 307208 | tf_op jit(solution)/shard_map/ppermute | solution.py:128
  86.8 10.3 %collective-permute-start.6 = (bf16[400,128]{1,0:T(8,128)(2,1)S(1)}, bf16[400,128]{1,0:T(8,128)(2,1)S(1)}, u32[]{:S(2)}, u32[]{:S(2)}) collective-permute-start(bf16[400,128]{1,0:T(8,128)(2,1)S(1)} %get-tuple-element.34), channel_id=1, source_target_pairs={{0,8},{8,16},{16,24},{24,0},{1,9},{9,17},{17,25},{25,1},{2,10},{10... | collective-permute-start | bytes 307208 | tf_op jit(solution)/shard_map/ppermute | solution.py:128
  87.3 9.8 %collective-permute-start.7 = (bf16[400,128]{1,0:T(8,128)(2,1)S(1)}, bf16[400,128]{1,0:T(8,128)(2,1)S(1)}, u32[]{:S(2)}, u32[]{:S(2)}) collective-permute-start(bf16[400,128]{1,0:T(8,128)(2,1)S(1)} %get-tuple-element.34), channel_id=1, source_target_pairs={{0,24},{8,0},{16,8},{24,16},{1,25},{9,1},{17,9},{25,17},{2,26},{10... | collective-permute-start | bytes 307208 | tf_op jit(solution)/shard_map/ppermute | solution.py:128
  90.4 6.8 %collective-permute-start.8 = (bf16[400,128]{1,0:T(8,128)(2,1)S(1)}, bf16[400,128]{1,0:T(8,128)(2,1)S(1)}, u32[]{:S(2)}, u32[]{:S(2)}) collective-permute-start(bf16[400,128]{1,0:T(8,128)(2,1)S(1)} %get-tuple-element.34), channel_id=1, source_target_pairs={{0,16},{8,24},{16,0},{24,8},{1,17},{9,25},{17,1},{25,9},{2,18},{10... | collective-permute-start | bytes 307208 | tf_op jit(solution)/shard_map/ppermute | solution.py:128
  90.5 14.3 %collective-permute-start.1 = (bf16[4,72,256]{2,1,0:T(8,128)(2,1)S(1)}, bf16[4,72,256]{2,1,0:T(8,128)(2,1)S(1)}, u32[]{:S(2)}, u32[]{:S(2)}) collective-permute-start(bf16[4,72,256]{2,1,0:T(8,128)(2,1)S(1)} %maximum_maximum_fusion.1), channel_id=1, source_target_pairs={{0,128},{64,192},{128,0},{192,64},{1,129},{65,193},{129,1},{193,65... | collective-permute-start | bytes 442376 | tf_op jit(solution)/shard_map/ppermute | solution.py:233
  97.2 19.3 %collective-permute-start.12 = (bf16[4,400,128]{2,1,0:T(8,128)(2,1)S(1)}, bf16[4,400,128]{2,1,0:T(8,128)(2,1)S(1)}, u32[]{:S(2)}, u32[]{:S(2)}) collective-permute-start(bf16[4,400,128]{2,1,0:T(8,128)(2,1)S(1)} %pad_maximum_fusion.2.refs_0_), channel_id=1, source_target_pairs={{0,1},{1,2},{2,3},{3,0},{4,5},{5,6},{6,7},{7,4},{8,9},{9,10},{10,1... | collective-permute-start | bytes 1228808 | tf_op jit(solution)/shard_map/ppermute | solution.py:128
  99.9 10.8 %collective-permute-start.2 = (bf16[4,72,256]{2,1,0:T(8,128)(2,1)S(1)}, bf16[4,72,256]{2,1,0:T(8,128)(2,1)S(1)}, u32[]{:S(2)}, u32[]{:S(2)}) collective-permute-start(bf16[4,72,256]{2,1,0:T(8,128)(2,1)S(1)} %maximum_maximum_fusion.1), channel_id=1, source_target_pairs={{0,192},{64,0},{128,64},{192,128},{1,193},{65,1},{129,65},{193,129... | collective-permute-start | bytes 442376 | tf_op jit(solution)/shard_map/ppermute | solution.py:233
  104.8 8.7 %collective-permute-start.3 = (bf16[4,72,256]{2,1,0:T(8,128)(2,1)S(1)}, bf16[4,72,256]{2,1,0:T(8,128)(2,1)S(1)}, u32[]{:S(2)}, u32[]{:S(2)}) collective-permute-start(bf16[4,72,256]{2,1,0:T(8,128)(2,1)S(1)} %maximum_maximum_fusion.1), channel_id=1, source_target_pairs={{0,64},{64,128},{128,192},{192,0},{1,65},{65,129},{129,193},{193,1... | collective-permute-start | bytes 442376 | tf_op jit(solution)/shard_map/ppermute | solution.py:233
  113.9 5.3 %copy-start.10 = (f32[256,256]{1,0:T(8,128)}, f32[256,256]{1,0:T(8,128)S(1)}, u32[]{:S(2)}) copy-start(f32[256,256]{1,0:T(8,128)S(1)} %bitcast_add_fusion) | copy-start | bytes 786436
  114.0 5.3 %collective-permute-start.4 = (f32[256,256]{1,0:T(8,128)S(1)}, f32[256,256]{1,0:T(8,128)}, u32[]{:S(2)}, u32[]{:S(2)}) collective-permute-start(f32[256,256]{1,0:T(8,128)S(1)} %bitcast_add_fusion), channel_id=1, source_target_pairs={{0,32},{32,0},{1,33},{33,1},{2,34},{34,2},{3,35},{35,3},{4,36},{36... | collective-permute-start | bytes 786440 | tf_op jit(solution)/shard_map/ppermute | solution.py:209
  114.1 12.1 %collective-permute-start.13 = (bf16[4,400,128]{2,1,0:T(8,128)(2,1)S(1)}, bf16[4,400,128]{2,1,0:T(8,128)(2,1)S(1)}, u32[]{:S(2)}, u32[]{:S(2)}) collective-permute-start(bf16[4,400,128]{2,1,0:T(8,128)(2,1)S(1)} %pad_maximum_fusion.2.refs_0_), channel_id=1, source_target_pairs={{0,3},{1,0},{2,1},{3,2},{4,7},{5,4},{6,5},{7,6},{8,11},{9,8},{10,9... | collective-permute-start | bytes 1228808 | tf_op jit(solution)/shard_map/ppermute | solution.py:128
  114.1 20.6 %collective-permute-start.14 = (bf16[4,400,128]{2,1,0:T(8,128)(2,1)S(1)}, bf16[4,400,128]{2,1,0:T(8,128)(2,1)S(1)}, u32[]{:S(2)}, u32[]{:S(2)}) collective-permute-start(bf16[4,400,128]{2,1,0:T(8,128)(2,1)S(1)} %pad_maximum_fusion.2.refs_0_), channel_id=1, source_target_pairs={{0,2},{1,3},{2,0},{3,1},{4,6},{5,7},{6,4},{7,5},{8,10},{9,11},{10,... | collective-permute-start | bytes 1228808 | tf_op jit(solution)/shard_map/ppermute | solution.py:128
  116.0 21.4 %collective-permute-start.15 = (bf16[4,400,128]{2,1,0:T(8,128)(2,1)S(1)}, bf16[4,400,128]{2,1,0:T(8,128)(2,1)S(1)}, u32[]{:S(2)}, u32[]{:S(2)}) collective-permute-start(bf16[4,400,128]{2,1,0:T(8,128)(2,1)S(1)} %pad_maximum_fusion.3.refs_4_), channel_id=1, source_target_pairs={{0,8},{8,16},{16,24},{24,0},{1,9},{9,17},{17,25},{25,1},{2,10},{10... | collective-permute-start | bytes 1228808 | tf_op jit(solution)/shard_map/ppermute | solution.py:128
  116.5 20.9 %collective-permute-start.16 = (bf16[4,400,128]{2,1,0:T(8,128)(2,1)S(1)}, bf16[4,400,128]{2,1,0:T(8,128)(2,1)S(1)}, u32[]{:S(2)}, u32[]{:S(2)}) collective-permute-start(bf16[4,400,128]{2,1,0:T(8,128)(2,1)S(1)} %pad_maximum_fusion.3.refs_4_), channel_id=1, source_target_pairs={{0,24},{8,0},{16,8},{24,16},{1,25},{9,1},{17,9},{25,17},{2,26},{10... | collective-permute-start | bytes 1228808 | tf_op jit(solution)/shard_map/ppermute | solution.py:128
  119.3 18.9 %collective-permute-start.17 = (bf16[4,400,128]{2,1,0:T(8,128)(2,1)S(1)}, bf16[4,400,128]{2,1,0:T(8,128)(2,1)S(1)}, u32[]{:S(2)}, u32[]{:S(2)}) collective-permute-start(bf16[4,400,128]{2,1,0:T(8,128)(2,1)S(1)} %pad_maximum_fusion.3.refs_4_), channel_id=1, source_target_pairs={{0,16},{8,24},{16,0},{24,8},{1,17},{9,25},{17,1},{25,9},{2,18},{10... | collective-permute-start | bytes 1228808 | tf_op jit(solution)/shard_map/ppermute | solution.py:128
  137.4 0.8 copy-start.3
  138.2 0.7 copy-start.5
  138.9 1.0 copy-start.4
  139.9 1.0 copy-start.6
  149.8 2.0 collective-permute-start.18
  152.4 8.4 %collective-permute-start.19 = (bf16[1,72,512]{2,1,0:T(8,128)(2,1)S(1)}, bf16[1,72,512]{2,1,0:T(8,128)(2,1)S(1)}, u32[]{:S(2)}, u32[]{:S(2)}) collective-permute-start(bf16[1,72,512]{2,1,0:T(8,128)(2,1)S(1)} %get-tuple-element.30), channel_id=1, source_target_pairs={{0,128},{64,192},{128,0},{192,64},{1,129},{65,193},{129,1},{193,65... | collective-permute-start | bytes 221192 | tf_op jit(solution)/shard_map/ppermute | solution.py:248
  155.0 28.8 %copy-start.1 = (f32[2048,512]{1,0:T(8,128)S(1)}, f32[2048,512]{1,0:T(8,128)}, u32[]{:S(2)}) copy-start(f32[2048,512]{1,0:T(8,128)} %basis.3) | copy-start | bytes 12582916
  155.0 10.4 %collective-permute-start.20 = (bf16[1,72,512]{2,1,0:T(8,128)(2,1)S(1)}, bf16[1,72,512]{2,1,0:T(8,128)(2,1)S(1)}, u32[]{:S(2)}, u32[]{:S(2)}) collective-permute-start(bf16[1,72,512]{2,1,0:T(8,128)(2,1)S(1)} %get-tuple-element.32), channel_id=1, source_target_pairs={{0,192},{64,0},{128,64},{192,128},{1,193},{65,1},{129,65},{193,129... | collective-permute-start | bytes 221192 | tf_op jit(solution)/shard_map/ppermute | solution.py:248
  158.0 7.5 %collective-permute-start.21 = (bf16[1,72,512]{2,1,0:T(8,128)(2,1)S(1)}, bf16[1,72,512]{2,1,0:T(8,128)(2,1)S(1)}, u32[]{:S(2)}, u32[]{:S(2)}) collective-permute-start(bf16[1,72,512]{2,1,0:T(8,128)(2,1)S(1)} %get-tuple-element.31), channel_id=1, source_target_pairs={{0,64},{64,128},{128,192},{192,0},{1,65},{65,129},{129,193},{193,1... | collective-permute-start | bytes 221192 | tf_op jit(solution)/shard_map/ppermute | solution.py:248
  181.4 2.0 collective-permute-start.22
  189.8 38.8 %copy-start.11 = (bf16[64,512]{1,0:T(8,128)(2,1)S(1)}, bf16[64,512]{1,0:T(8,128)(2,1)}, u32[]{:S(2)}) copy-start(bf16[64,512]{1,0:T(8,128)(2,1)} %param.12) | copy-start | bytes 196612

commit v5 on v4

--- a/solution.py
+++ b/solution.py
@@ -346,7 +346,15 @@
         ),
         compiler_params=pltpu.CompilerParams(vmem_limit_bytes=12 * 2**20),
         name="apply_piece",
-    )(place, left, pltpu.with_memory_space_constraint(eig_damped, pltpu.HBM), *pieces)
+    )(
+        place,
+        left,
+        pltpu.with_memory_space_constraint(eig_damped, pltpu.HBM),
+        *(
+            pltpu.with_memory_space_constraint(piece, pltpu.HBM) if k % 4 == 0 else piece
+            for k, piece in enumerate(pieces)
+        ),
+    )
     applied = both_halves(summed_in_turn(my_half_summed(contrib, core)), core)
     response = jnp.concatenate(respond_to(basis_out, applied), axis=1)
     scores = jnp.sum(train_left.astype(f32) * response, axis=0).reshape(-1, 128)

time: 256 us -> 253 us (0.988)
  local copies, waits for them, and re-layouts: 11.2 us -> 7.65 us
    unnamed x28 -> x18, local copies, waits for them, and re-layouts: 8.23 us -> 4.72 us
  transfers between devices with their start and end apart: 23 -> 23, of which waited for: 9 -> 8; matrix products, arithmetic and copies ran while one was open for 3% -> 3% of each run, Pallas kernels for 0% -> 0%
where the time goes in v5:
time: 253 us; the launch traced here: 251 us
  blocking collectives  137 us (54%)
  waiting for transfers between devices  35.4 us (14%)
  starting transfers between devices  34.3 us (14%)
  Pallas kernels  24.6 us (10%)
  other arithmetic  9.47 us (4%)
  local copies, waits for them, and re-layouts  7.65 us (3%)
    all_to_all x4, blocking collectives, exchange(): return lax.all_to_all(pieces, axis, split_axis=0, concat_axis=0, tiled=True)  122 us
    ppermute x12, waiting for transfers between devices, around(): lax.ppermute(array, axis, ring(axis, 4 - k))  17.3 us
    pallas_call x2, Pallas kernels, call(): pl.pallas_call(kernel, out_shape=out, grid=(grid,), in_specs=ins, out_spe...  15.2 us
    ppermute x12, starting transfers between devices, around(): lax.ppermute(array, axis, ring(axis, 4 - k))  15.1 us
    all_gather x1, blocking collectives, summed_in_turn(): lax.all_gather(coded_columns(total, 8), 'row_0', axis=0, tiled=True)  14.2 us
    ppermute x3, starting transfers between devices, summed_over_chips(): arrived.append(lax.ppermute(message, 'row_0', ring('row_0', step)))  10.7 us
    pallas_call x1, Pallas kernels, body(): pl.pallas_call(apply_piece, out_shape=struct((n_out, train), f32), in_spe...  9.42 us
    ppermute x3, waiting for transfers between devices, summed_over_chips(): arrived.append(lax.ppermute(message, 'row_0', ring('row_0', step)))  8.41 us
  transfers between devices with their start and end apart: 23, of which 8 were waited for; matrix products, arithmetic and copies ran while one was open for 3% of the time, Pallas kernels for 0%

profile of v5, /device:TPU:8, one launch (start us, length us, event | category | flops | bytes accessed | tf_op | source)
XLA Modules:
  0.0 251.0 jit_solution(14670241688133881660)
XLA Ops:
  0.6 1.0 copy-done.2
  1.7 0.9 copy-done.3
  2.6 0.8 copy-done.4
  3.4 9.2 %shard_map.86 = bf16[4,2,4,528,128]{4,3,2,1,0:T(8,128)(2,1)S(1)} custom-call(f32[512,2048]{1,0:T(8,128)} %basis.2, bf16[512,256]{1,0:T(8,128)(2,1)S(1)} %copy-done.3, bf16[512,512]{1,0:T(8,128)(2,1)S(1)} %copy-done.2, bf16[64,256]{1,0:T(8,128)(2,1)S(1)} %copy-done.4), custom_call_target="tpu_custom_call" | custom-call | flops 3221225472 | bytes 5013504 | tf_op jit(solution)/shard_map/pallas_call | solution.py:104
  12.6 60.5 %all_to_all.20 = bf16[32,528,128]{2,1,0:T(8,128)(2,1)S(1)} all-to-all(bf16[32,528,128]{2,1,0:T(8,128)(2,1)S(1)} %bitcast.114), channel_id=1, replica_groups=mesh['row_0'=4,'row_1'=2,'col_0'=4,'col_1'=2,'col_2'=4] {'col_0','col_1'..., dimensions={0} | all-to-all | bytes 8650752 | tf_op jit(solution)/shard_map/all_to_all | solution.py:21
  73.2 1.9 copy-done.5
  75.1 2.4 fusion.4
  77.7 0.8 collective-permute-start.5
  78.5 1.6 slice.103
  80.1 1.1 copy.17
  81.2 0.7 fusion.11
  82.0 1.0 fusion.15
  83.0 0.1 collective-permute-start
  83.2 0.1 collective-permute-start.9
  83.3 2.0 collective-permute-start.10
  85.3 1.5 collective-permute-start.11
  86.8 0.5 collective-permute-start.6
  87.3 2.7 %collective-permute-start.7 = (bf16[400,128]{1,0:T(8,128)(2,1)S(1)}, bf16[400,128]{1,0:T(8,128)(2,1)S(1)}, u32[]{:S(2)}, u32[]{:S(2)}) collective-permute-start(bf16[400,128]{1,0:T(8,128)(2,1)S(1)} %get-tuple-element.34), channel_id=1, source_target_pairs={{0,24},{8,0},{16,8},{24,16},{1,25},{9,1},{17,9},{25,17},{2,26},{10... | collective-permute-start | bytes 307208 | tf_op jit(solution)/shard_map/ppermute | solution.py:128
  90.2 0.1 fusion.42
  90.3 0.1 maximum_maximum_fusion.1
  90.4 0.1 collective-permute-start.8
  90.5 6.6 %collective-permute-start.1 = (bf16[4,72,256]{2,1,0:T(8,128)(2,1)S(1)}, bf16[4,72,256]{2,1,0:T(8,128)(2,1)S(1)}, u32[]{:S(2)}, u32[]{:S(2)}) collective-permute-start(bf16[4,72,256]{2,1,0:T(8,128)(2,1)S(1)} %maximum_maximum_fusion.1), channel_id=1, source_target_pairs={{0,128},{64,192},{128,0},{192,64},{1,129},{65,193},{129,1},{193,65... | collective-permute-start | bytes 442376 | tf_op jit(solution)/shard_map/ppermute | solution.py:233
  97.0 0.8 pad_maximum_fusion.3.refs_4_
  97.9 0.8 pad_maximum_fusion.2.refs_0_
  98.7 2.6 %collective-permute-start.12 = (bf16[4,400,128]{2,1,0:T(8,128)(2,1)}, bf16[4,400,128]{2,1,0:T(8,128)(2,1)S(1)}, u32[]{:S(2)}, u32[]{:S(2)}) collective-permute-start(bf16[4,400,128]{2,1,0:T(8,128)(2,1)} %pad_maximum_fusion.2.refs_0_), channel_id=1, source_target_pairs={{0,1},{1,2},{2,3},{3,0},{4,5},{5,6},{6,7},{7,4},{8,9},{9,10},{10,1... | collective-permute-start | bytes 1228808 | tf_op jit(solution)/shard_map/ppermute | solution.py:128
  101.3 4.2 %collective-permute-start.2 = (bf16[4,72,256]{2,1,0:T(8,128)(2,1)S(1)}, bf16[4,72,256]{2,1,0:T(8,128)(2,1)S(1)}, u32[]{:S(2)}, u32[]{:S(2)}) collective-permute-start(bf16[4,72,256]{2,1,0:T(8,128)(2,1)S(1)} %maximum_maximum_fusion.1), channel_id=1, source_target_pairs={{0,192},{64,0},{128,64},{192,128},{1,193},{65,1},{129,65},{193,129... | collective-permute-start | bytes 442376 | tf_op jit(solution)/shard_map/ppermute | solution.py:233
  105.5 5.1 %collective-permute-done.2 = bf16[4,72,256]{2,1,0:T(8,128)(2,1)S(1)} collective-permute-done((bf16[4,72,256]{2,1,0:T(8,128)(2,1)S(1)}, bf16[4,72,256]{2,1,0:T(8,128)(2,1)S(1)}, u32[]{:S(2)}, u32[]{:S(2)}) %collective-permute-start.2) | collective-permute-done | bytes 147488 | tf_op jit(solution)/shard_map/ppermute | solution.py:233
  110.6 3.3 %collective-permute-done.3 = bf16[4,72,256]{2,1,0:T(8,128)(2,1)S(1)} collective-permute-done((bf16[4,72,256]{2,1,0:T(8,128)(2,1)S(1)}, bf16[4,72,256]{2,1,0:T(8,128)(2,1)S(1)}, u32[]{:S(2)}, u32[]{:S(2)}) %collective-permute-start.3) | collective-permute-done | bytes 147488 | tf_op jit(solution)/shard_map/ppermute | solution.py:233
  114.0 0.1 negate_select_fusion.6
  114.1 0.1 negate_select_fusion.5
  114.2 0.1 negate_select_fusion.4
  114.4 0.1 collective-permute-start.4
  114.6 1.4 collective-permute-start.14
  116.0 0.5 collective-permute-start.15
  116.5 2.8 %collective-permute-start.16 = (bf16[4,400,128]{2,1,0:T(8,128)(2,1)}, bf16[4,400,128]{2,1,0:T(8,128)(2,1)S(1)}, u32[]{:S(2)}, u32[]{:S(2)}) collective-permute-start(bf16[4,400,128]{2,1,0:T(8,128)(2,1)} %pad_maximum_fusion.3.refs_4_), channel_id=1, source_target_pairs={{0,24},{8,0},{16,8},{24,16},{1,25},{9,1},{17,9},{25,17},{2,26},{10... | collective-permute-start | bytes 1228808 | tf_op jit(solution)/shard_map/ppermute | solution.py:128
  119.3 0.8 collective-permute-start.17
  120.2 0.1 fusion.25
  120.3 15.0 %collective-permute-done.13.refs_2_ = bf16[4,400,128]{2,1,0:T(8,128)(2,1)S(1)} collective-permute-done((bf16[4,400,128]{2,1,0:T(8,128)(2,1)}, bf16[4,400,128]{2,1,0:T(8,128)(2,1)S(1)}, u32[]{:S(2)}, u32[]{:S(2)}) %collective-permute-start.13) | collective-permute-done | bytes 409632 | tf_op jit(solution)/shard_map/ppermute | solution.py:128
  135.3 2.3 collective-permute-done.15.refs_5_
  137.6 9.4 %apply_piece.1 = f32[512,512]{1,0:T(8,128)S(1)} custom-call(s32[2]{0:T(128)S(1)} %pad_add_fusion.place, bf16[512,768]{1,0:T(8,128)(2,1)S(1)} %pad_maximum_fusion.1.left, f32[512,2048]{1,0:T(8,128)} %eig.1, bf16[4,400,128]{2,1,0:T(8,128)(2,1)} %pad_maximum_fusion.2.refs_0_, bf16[4,400,128]{2,1,0:T(8,128)(2,1)S(1)} %collective-permute-done.12.refs_1_, ...), custom_call_target="tpu_custom_call" | custom-call | flops 4831838208 | bytes 4194304 | tf_op jit(solution)/shard_map/apply_piece/pallas_call | solution.py:331
  147.1 0.1 collective-permute-start.18
  147.2 1.9 collective-permute-done.18
  149.1 0.1 broadcast_compare_fusion
  149.3 0.2 fusion.26
  149.5 0.1 maximum_maximum_fusion
  149.7 4.4 %collective-permute-start.19 = (bf16[1,72,512]{2,1,0:T(8,128)(2,1)S(1)}, bf16[1,72,512]{2,1,0:T(8,128)(2,1)S(1)}, u32[]{:S(2)}, u32[]{:S(2)}) collective-permute-start(bf16[1,72,512]{2,1,0:T(8,128)(2,1)S(1)} %get-tuple-element.30), channel_id=1, source_target_pairs={{0,128},{64,192},{128,0},{192,64},{1,129},{65,193},{129,1},{193,65... | collective-permute-start | bytes 221192 | tf_op jit(solution)/shard_map/ppermute | solution.py:248
  154.1 1.2 collective-permute-start.20
  155.2 1.7 collective-permute-start.21
  157.0 1.1 collective-permute-done.19
  158.1 4.8 %collective-permute-done.20 = bf16[1,72,512]{2,1,0:T(8,128)(2,1)S(1)} collective-permute-done((bf16[1,72,512]{2,1,0:T(8,128)(2,1)S(1)}, bf16[1,72,512]{2,1,0:T(8,128)(2,1)S(1)}, u32[]{:S(2)}, u32[]{:S(2)}) %collective-permute-start.20) | collective-permute-done | bytes 73760 | tf_op jit(solution)/shard_map/ppermute | solution.py:248
  163.0 0.2 abs_reduce_fusion
  163.3 14.2 %all_gather.3 = bf16[4,72,512]{2,1,0:T(8,128)(2,1)S(1)} all-gather(bf16[1,72,512]{2,1,0:T(8,128)(2,1)S(1)} %maximum_maximum_fusion.2), channel_id=1, replica_groups=mesh['row_0'=4,'row_1'=2,'col_0'=4,'col_1'=2,'col_2'=4] {'row_0'}, dimensions={0}, use_global_device_ids=true | all-gather | bytes 368640 | tf_op jit(solution)/shard_map/all_gather | solution.py:251
  177.6 0.2 negate_select_fusion.2
  177.8 0.1 collective-permute-start.22
  177.9 1.9 collective-permute-done.22
  179.8 0.2 reduce-precision_convert_fusion.2
  180.0 0.1 pad_maximum_fusion.given
  180.2 6.0 %shard_map.87 = bf16[32,264,128]{2,1,0:T(8,128)(2,1)S(1)} custom-call(f32[2048,512]{1,0:T(8,128)S(1)} %copy-done.1, bf16[1536,512]{1,0:T(8,128)(2,1)S(1)} %pad_maximum_fusion.given), custom_call_target="tpu_custom_call" | custom-call | flops 3221225472 | bytes 5767168 | tf_op jit(solution)/shard_map/pallas_call | solution.py:104
  186.2 38.2 %all_to_all.21 = bf16[32,264,128]{2,1,0:T(8,128)(2,1)S(1)} all-to-all(bf16[32,264,128]{2,1,0:T(8,128)(2,1)S(1)} %shard_map.87), channel_id=1, replica_groups=mesh['row_0'=4,'row_1'=2,'col_0'=4,'col_1'=2,'col_2'=4] {'col_0','col_1'..., dimensions={0} | all-to-all | bytes 4325376 | tf_op jit(solution)/shard_map/all_to_all | solution.py:21
  224.4 1.5 fusion.10
  226.0 0.7 multiply_reduce_fusion
  226.7 11.8 %all_to_all.22 = f32[32,4,128]{2,1,0:T(4,128)S(1)} all-to-all(f32[32,4,128]{2,1,0:T(4,128)S(1)} %broadcast_in_dim.13), channel_id=1, replica_groups=mesh['row_0'=4,'row_1'=2,'col_0'=4,'col_1'=2,'col_2'=4] {'col_0','col_1'..., dimensions={0} | all-to-all | bytes 131072 | tf_op jit(solution)/shard_map/all_to_all | solution.py:21
  238.5 11.9 %all_to_all.23 = f32[8,4,128]{2,1,0:T(4,128)S(1)} all-to-all(f32[8,4,128]{2,1,0:T(4,128)S(1)} %broadcast_in_dim.14), channel_id=1, replica_groups=mesh['row_0'=4,'row_1'=2,'col_0'=4,'col_1'=2,'col_2'=4] {'row_0','row_1'}, dimensions={0} | all-to-all | bytes 32768 | tf_op jit(solution)/shard_map/all_to_all | solution.py:21
  250.4 0.6 reduce_sum.49
  (69 shorter events, 1.3 us)
Async XLA Ops:
  0.6 1.0 copy-start.2
  1.7 0.9 copy-start.3
  2.6 0.8 copy-start.4
  73.1 2.0 copy-start.5
  77.6 3.7 %copy-start = (f32[2048,512]{1,0:T(8,128)S(1)}, f32[2048,512]{1,0:T(8,128)}, u32[]{:S(2)}) copy-start(f32[2048,512]{1,0:T(8,128)} %basis.3) | copy-start | bytes 12582916
  77.7 5.5 %collective-permute-start.5 = (bf16[400,128]{1,0:T(8,128)(2,1)S(1)}, bf16[400,128]{1,0:T(8,128)(2,1)S(1)}, u32[]{:S(2)}, u32[]{:S(2)}) collective-permute-start(bf16[400,128]{1,0:T(8,128)(2,1)S(1)} %fusion.73), channel_id=1, source_target_pairs={{0,4},{4,0},{1,5},{5,1},{2,6},{6,2},{3,7},{7,3},{8,12},{12,8},{9,1... | collective-permute-start | bytes 307208 | tf_op jit(solution)/shard_map/ppermute | solution.py:313
  83.0 4.3 %collective-permute-start = (f32[256,256]{1,0:T(8,128)S(1)}, f32[256,256]{1,0:T(8,128)S(1)}, u32[]{:S(2)}, u32[]{:S(2)}) collective-permute-start(f32[256,256]{1,0:T(8,128)S(1)} %constant_dynamic-slice_fusion.4), channel_id=1, source_target_pairs={{0,32},{32,0},{1,33},{33,1},{2,34},{34,2},{3,35},{35,3},{4,36},{36... | collective-permute-start | bytes 786440 | tf_op jit(solution)/shard_map/ppermute | solution.py:205
  83.2 7.1 %collective-permute-start.9 = (bf16[400,128]{1,0:T(8,128)(2,1)S(1)}, bf16[400,128]{1,0:T(8,128)(2,1)S(1)}, u32[]{:S(2)}, u32[]{:S(2)}) collective-permute-start(bf16[400,128]{1,0:T(8,128)(2,1)S(1)} %get-tuple-element.33), channel_id=1, source_target_pairs={{0,1},{1,2},{2,3},{3,0},{4,5},{5,6},{6,7},{7,4},{8,9},{9,10},{10,1... | collective-permute-start | bytes 307208 | tf_op jit(solution)/shard_map/ppermute | solution.py:128
  83.3 7.2 %collective-permute-start.10 = (bf16[400,128]{1,0:T(8,128)(2,1)S(1)}, bf16[400,128]{1,0:T(8,128)(2,1)S(1)}, u32[]{:S(2)}, u32[]{:S(2)}) collective-permute-start(bf16[400,128]{1,0:T(8,128)(2,1)S(1)} %get-tuple-element.33), channel_id=1, source_target_pairs={{0,3},{1,0},{2,1},{3,2},{4,7},{5,4},{6,5},{7,6},{8,11},{9,8},{10,9... | collective-permute-start | bytes 307208 | tf_op jit(solution)/shard_map/ppermute | solution.py:128
  85.3 11.7 %collective-permute-start.11 = (bf16[400,128]{1,0:T(8,128)(2,1)S(1)}, bf16[400,128]{1,0:T(8,128)(2,1)S(1)}, u32[]{:S(2)}, u32[]{:S(2)}) collective-permute-start(bf16[400,128]{1,0:T(8,128)(2,1)S(1)} %get-tuple-element.33), channel_id=1, source_target_pairs={{0,2},{1,3},{2,0},{3,1},{4,6},{5,7},{6,4},{7,5},{8,10},{9,11},{10,... | collective-permute-start | bytes 307208 | tf_op jit(solution)/shard_map/ppermute | solution.py:128
  86.8 11.1 %collective-permute-start.6 = (bf16[400,128]{1,0:T(8,128)(2,1)S(1)}, bf16[400,128]{1,0:T(8,128)(2,1)S(1)}, u32[]{:S(2)}, u32[]{:S(2)}) collective-permute-start(bf16[400,128]{1,0:T(8,128)(2,1)S(1)} %get-tuple-element.34), channel_id=1, source_target_pairs={{0,8},{8,16},{16,24},{24,0},{1,9},{9,17},{17,25},{25,1},{2,10},{10... | collective-permute-start | bytes 307208 | tf_op jit(solution)/shard_map/ppermute | solution.py:128
  87.3 10.6 %collective-permute-start.7 = (bf16[400,128]{1,0:T(8,128)(2,1)S(1)}, bf16[400,128]{1,0:T(8,128)(2,1)S(1)}, u32[]{:S(2)}, u32[]{:S(2)}) collective-permute-start(bf16[400,128]{1,0:T(8,128)(2,1)S(1)} %get-tuple-element.34), channel_id=1, source_target_pairs={{0,24},{8,0},{16,8},{24,16},{1,25},{9,1},{17,9},{25,17},{2,26},{10... | collective-permute-start | bytes 307208 | tf_op jit(solution)/shard_map/ppermute | solution.py:128
  90.4 7.5 %collective-permute-start.8 = (bf16[400,128]{1,0:T(8,128)(2,1)S(1)}, bf16[400,128]{1,0:T(8,128)(2,1)S(1)}, u32[]{:S(2)}, u32[]{:S(2)}) collective-permute-start(bf16[400,128]{1,0:T(8,128)(2,1)S(1)} %get-tuple-element.34), channel_id=1, source_target_pairs={{0,16},{8,24},{16,0},{24,8},{1,17},{9,25},{17,1},{25,9},{2,18},{10... | collective-permute-start | bytes 307208 | tf_op jit(solution)/shard_map/ppermute | solution.py:128
  90.5 15.0 %collective-permute-start.1 = (bf16[4,72,256]{2,1,0:T(8,128)(2,1)S(1)}, bf16[4,72,256]{2,1,0:T(8,128)(2,1)S(1)}, u32[]{:S(2)}, u32[]{:S(2)}) collective-permute-start(bf16[4,72,256]{2,1,0:T(8,128)(2,1)S(1)} %maximum_maximum_fusion.1), channel_id=1, source_target_pairs={{0,128},{64,192},{128,0},{192,64},{1,129},{65,193},{129,1},{193,65... | collective-permute-start | bytes 442376 | tf_op jit(solution)/shard_map/ppermute | solution.py:233
  98.7 17.8 %collective-permute-start.12 = (bf16[4,400,128]{2,1,0:T(8,128)(2,1)}, bf16[4,400,128]{2,1,0:T(8,128)(2,1)S(1)}, u32[]{:S(2)}, u32[]{:S(2)}) collective-permute-start(bf16[4,400,128]{2,1,0:T(8,128)(2,1)} %pad_maximum_fusion.2.refs_0_), channel_id=1, source_target_pairs={{0,1},{1,2},{2,3},{3,0},{4,5},{5,6},{6,7},{7,4},{8,9},{9,10},{10,1... | collective-permute-start | bytes 1228808 | tf_op jit(solution)/shard_map/ppermute | solution.py:128
  101.3 9.3 %collective-permute-start.2 = (bf16[4,72,256]{2,1,0:T(8,128)(2,1)S(1)}, bf16[4,72,256]{2,1,0:T(8,128)(2,1)S(1)}, u32[]{:S(2)}, u32[]{:S(2)}) collective-permute-start(bf16[4,72,256]{2,1,0:T(8,128)(2,1)S(1)} %maximum_maximum_fusion.1), channel_id=1, source_target_pairs={{0,192},{64,0},{128,64},{192,128},{1,193},{65,1},{129,65},{193,129... | collective-permute-start | bytes 442376 | tf_op jit(solution)/shard_map/ppermute | solution.py:233
  105.5 8.5 %collective-permute-start.3 = (bf16[4,72,256]{2,1,0:T(8,128)(2,1)S(1)}, bf16[4,72,256]{2,1,0:T(8,128)(2,1)S(1)}, u32[]{:S(2)}, u32[]{:S(2)}) collective-permute-start(bf16[4,72,256]{2,1,0:T(8,128)(2,1)S(1)} %maximum_maximum_fusion.1), channel_id=1, source_target_pairs={{0,64},{64,128},{128,192},{192,0},{1,65},{65,129},{129,193},{193,1... | collective-permute-start | bytes 442376 | tf_op jit(solution)/shard_map/ppermute | solution.py:233
  114.4 4.9 %collective-permute-start.4 = (f32[256,256]{1,0:T(8,128)S(1)}, f32[256,256]{1,0:T(8,128)S(1)}, u32[]{:S(2)}, u32[]{:S(2)}) collective-permute-start(f32[256,256]{1,0:T(8,128)S(1)} %bitcast_add_fusion), channel_id=1, source_target_pairs={{0,32},{32,0},{1,33},{33,1},{2,34},{34,2},{3,35},{35,3},{4,36},{36... | collective-permute-start | bytes 786440 | tf_op jit(solution)/shard_map/ppermute | solution.py:209
  114.5 20.9 %collective-permute-start.13 = (bf16[4,400,128]{2,1,0:T(8,128)(2,1)}, bf16[4,400,128]{2,1,0:T(8,128)(2,1)S(1)}, u32[]{:S(2)}, u32[]{:S(2)}) collective-permute-start(bf16[4,400,128]{2,1,0:T(8,128)(2,1)} %pad_maximum_fusion.2.refs_0_), channel_id=1, source_target_pairs={{0,3},{1,0},{2,1},{3,2},{4,7},{5,4},{6,5},{7,6},{8,11},{9,8},{10,9... | collective-permute-start | bytes 1228808 | tf_op jit(solution)/shard_map/ppermute | solution.py:128
  114.6 20.8 %collective-permute-start.14 = (bf16[4,400,128]{2,1,0:T(8,128)(2,1)}, bf16[4,400,128]{2,1,0:T(8,128)(2,1)S(1)}, u32[]{:S(2)}, u32[]{:S(2)}) collective-permute-start(bf16[4,400,128]{2,1,0:T(8,128)(2,1)} %pad_maximum_fusion.2.refs_0_), channel_id=1, source_target_pairs={{0,2},{1,3},{2,0},{3,1},{4,6},{5,7},{6,4},{7,5},{8,10},{9,11},{10,... | collective-permute-start | bytes 1228808 | tf_op jit(solution)/shard_map/ppermute | solution.py:128
  116.0 21.6 %collective-permute-start.15 = (bf16[4,400,128]{2,1,0:T(8,128)(2,1)}, bf16[4,400,128]{2,1,0:T(8,128)(2,1)S(1)}, u32[]{:S(2)}, u32[]{:S(2)}) collective-permute-start(bf16[4,400,128]{2,1,0:T(8,128)(2,1)} %pad_maximum_fusion.3.refs_4_), channel_id=1, source_target_pairs={{0,8},{8,16},{16,24},{24,0},{1,9},{9,17},{17,25},{25,1},{2,10},{10... | collective-permute-start | bytes 1228808 | tf_op jit(solution)/shard_map/ppermute | solution.py:128
  116.5 21.1 %collective-permute-start.16 = (bf16[4,400,128]{2,1,0:T(8,128)(2,1)}, bf16[4,400,128]{2,1,0:T(8,128)(2,1)S(1)}, u32[]{:S(2)}, u32[]{:S(2)}) collective-permute-start(bf16[4,400,128]{2,1,0:T(8,128)(2,1)} %pad_maximum_fusion.3.refs_4_), channel_id=1, source_target_pairs={{0,24},{8,0},{16,8},{24,16},{1,25},{9,1},{17,9},{25,17},{2,26},{10... | collective-permute-start | bytes 1228808 | tf_op jit(solution)/shard_map/ppermute | solution.py:128
  119.3 18.4 %collective-permute-start.17 = (bf16[4,400,128]{2,1,0:T(8,128)(2,1)}, bf16[4,400,128]{2,1,0:T(8,128)(2,1)S(1)}, u32[]{:S(2)}, u32[]{:S(2)}) collective-permute-start(bf16[4,400,128]{2,1,0:T(8,128)(2,1)} %pad_maximum_fusion.3.refs_4_), channel_id=1, source_target_pairs={{0,16},{8,24},{16,0},{24,8},{1,17},{9,25},{17,1},{25,9},{2,18},{10... | collective-permute-start | bytes 1228808 | tf_op jit(solution)/shard_map/ppermute | solution.py:128
  147.1 2.0 collective-permute-start.18
  149.7 8.4 %collective-permute-start.19 = (bf16[1,72,512]{2,1,0:T(8,128)(2,1)S(1)}, bf16[1,72,512]{2,1,0:T(8,128)(2,1)S(1)}, u32[]{:S(2)}, u32[]{:S(2)}) collective-permute-start(bf16[1,72,512]{2,1,0:T(8,128)(2,1)S(1)} %get-tuple-element.30), channel_id=1, source_target_pairs={{0,128},{64,192},{128,0},{192,64},{1,129},{65,193},{129,1},{193,65... | collective-permute-start | bytes 221192 | tf_op jit(solution)/shard_map/ppermute | solution.py:248
  154.1 26.1 %copy-start.1 = (f32[2048,512]{1,0:T(8,128)S(1)}, f32[2048,512]{1,0:T(8,128)}, u32[]{:S(2)}) copy-start(f32[2048,512]{1,0:T(8,128)} %basis.3) | copy-start | bytes 12582916
  154.1 8.9 %collective-permute-start.20 = (bf16[1,72,512]{2,1,0:T(8,128)(2,1)S(1)}, bf16[1,72,512]{2,1,0:T(8,128)(2,1)S(1)}, u32[]{:S(2)}, u32[]{:S(2)}) collective-permute-start(bf16[1,72,512]{2,1,0:T(8,128)(2,1)S(1)} %get-tuple-element.32), channel_id=1, source_target_pairs={{0,192},{64,0},{128,64},{192,128},{1,193},{65,1},{129,65},{193,129... | collective-permute-start | bytes 221192 | tf_op jit(solution)/shard_map/ppermute | solution.py:248
  155.2 7.7 %collective-permute-start.21 = (bf16[1,72,512]{2,1,0:T(8,128)(2,1)S(1)}, bf16[1,72,512]{2,1,0:T(8,128)(2,1)S(1)}, u32[]{:S(2)}, u32[]{:S(2)}) collective-permute-start(bf16[1,72,512]{2,1,0:T(8,128)(2,1)S(1)} %get-tuple-element.31), channel_id=1, source_target_pairs={{0,64},{64,128},{128,192},{192,0},{1,65},{65,129},{129,193},{193,1... | collective-permute-start | bytes 221192 | tf_op jit(solution)/shard_map/ppermute | solution.py:248
  177.8 2.0 collective-permute-start.22
  186.2 39.8 %copy-start.6 = (bf16[64,512]{1,0:T(8,128)(2,1)S(1)}, bf16[64,512]{1,0:T(8,128)(2,1)}, u32[]{:S(2)}) copy-start(bf16[64,512]{1,0:T(8,128)(2,1)} %param.12) | copy-start | bytes 196612
